TPU v7x, 32 devices: a whole 2x2x4 slice. The times are simulated.
32 devices in a mesh: slab: 8 (over z, x), freq: 4 (over y, core).
Axes of the slice: x: 2, y: 2, z: 4, core: 2. Of those that a mesh axis runs over, the one named last changes fastest.
Arguments:
- partials: bfloat16 [8, 3, 2, 32, 32, 5, 256], P('slab', None, None, 'freq'), may hold values from -400 to 400
- rec_plane: int32 [8, 3, 2], P('slab'), may hold values from 0 to 1
- rec_count: int32 [8, 3], P('slab'), may hold values from 0 to 2, as said below
- rec_weight: bfloat16 [8, 3, 2, 256], P('slab'), may hold values from 0.25 to 1
- qweight: float32 [16, 256], P('slab'), as said below
Outputs:
- spectra: bfloat16 [8, 32, 2, 16, 5, 256], P('freq', None, None, 'slab')
- r_factor: float32 [8, 64, 64], P('freq')
Inputs may be any that keep to these rules, and one draw needn't show every extreme that they name: `rec_count`: at most 2 live records from one source to one destination, reached in every draw; a source's records to its own index number exactly 2; none leave the ends of the slab axis; some destination receives 2 from each of its three sources. `qweight`: positive.
All inputs are finite; a program needn't handle non-finite values.
Results may differ from a plain program's by a relative error of at most 0.0025.
The roundings to bfloat16 on the way count: a program that leaves them out, or rounds other values in their place, can miss the bound.
Values may be sent and summed in bfloat16 or wider, within the bound.
No kernel may reach another device: no remote copies, remote signals or barrier semaphores. Data moves between devices by JAX's collectives and lax.ppermute only.
A program may use at most 64 MiB of HBM per device.

v0:
```python
import math

import jax
import jax.numpy as jnp
from jax import lax
from jax.sharding import PartitionSpec as P

NT = 32
NY = 16
NZ = 16
NF = 8


TAPS = (-0.0625, 0.25, 0.625, 0.25, -0.0625)


def from_behind(value, axis, steps):
    count = lax.axis_size(axis)
    leading, last = (max(0, -steps), min(count, count - steps))
    return lax.ppermute(value, axis, [(source, source + steps) for source in range(leading, last)])


def padded_2(block, sides, width):
    for axis, dim in sides:
        count = lax.axis_size(axis)
        forward = [(i, i + 1) for i in range(count - 1)]
        backward = [(target, source) for source, target in forward]
        low = lax.ppermute(
            lax.slice_in_dim(block, block.shape[dim] - width, None, axis=dim), axis, forward
        )
        high = lax.ppermute(lax.slice_in_dim(block, 0, width, axis=dim), axis, backward)
        block = jnp.concatenate([low, block, high], axis=dim)
    return block


def band_matrix(size):
    index = jnp.arange(size)
    offset = index[None, :] - index[:, None]
    result = jnp.zeros((size, size), jnp.float32)
    for place in range(5):
        result = result + TAPS[place] * (offset == place - 2).astype(jnp.float32)
    return result


def dft_table():
    times = jnp.arange(NT).astype(jnp.float32)
    freqs = jnp.arange(NF).astype(jnp.float32) + 1.0
    window = 0.5 - 0.5 * jnp.cos(2.0 * math.pi * times / NT)
    factor = 1.0 / jnp.sqrt(jnp.sum(window * window))
    angle = 2.0 * math.pi * times[:, None] * freqs[None, :] / NT
    real_part = factor * window[:, None] * jnp.cos(angle)
    imag_part = -factor * window[:, None] * jnp.sin(angle)
    return jnp.stack([real_part, imag_part], axis=2)


def record_terms(pieces, weights, planes, counts, plane_total):
    slots = jnp.arange(pieces.shape[0])
    valid = slots < counts[0]
    select = ((planes[:, None] == jnp.arange(plane_total)[None, :]) & valid[:, None]).astype(
        jnp.float32
    )
    scaled = pieces.astype(jnp.float32) * weights.astype(jnp.float32)[:, None, None, None, :]
    return jnp.einsum("cq,cbtvp->qbtvp", select, scaled, precision=lax.Precision.HIGHEST)


def upper_factor(gram):
    return jnp.swapaxes(jnp.linalg.cholesky(gram), 1, 2)


def add_products(total, piece):
    return total + jnp.einsum("akij,akil->kjl", piece, piece, precision=lax.Precision.HIGHEST)


def body(partials, rec_plane, rec_count, rec_weight, qweight):
    plane_total = qweight.shape[0]
    points = qweight.shape[1]

    def side_terms(side):
        return record_terms(
            partials[0, side],
            rec_weight[0, side],
            rec_plane[0, side],
            rec_count[0, side : side + 1],
            plane_total,
        )

    total = side_terms(1)
    total = total + from_behind(side_terms(0), "slab", -1)
    total = total + from_behind(side_terms(2), "slab", 1)
    assembled = total.astype(jnp.bfloat16)
    padded = padded_2(assembled, (("slab", 0),), 2)
    kyz = jnp.kron(band_matrix(NY), band_matrix(NZ)).astype(jnp.bfloat16)
    across = jnp.dot(padded.reshape(-1, points), kyz, preferred_element_type=jnp.float32).reshape(
        padded.shape
    )
    smoothed = TAPS[0] * across[0:plane_total]
    for place in range(1, 5):
        smoothed = smoothed + TAPS[place] * across[place : place + plane_total]
    local_spec = jnp.einsum(
        "xbtvp,tkr->kbrxvp", smoothed, dft_table(), precision=lax.Precision.HIGHEST
    ).astype(jnp.bfloat16)
    spectra = lax.all_to_all(local_spec, "freq", split_axis=0, concat_axis=1, tiled=True)
    freq_count = spectra.shape[0]
    columns = 2 * spectra.shape[1]
    values = spectra.astype(jnp.float32).reshape(
        freq_count, columns, plane_total, spectra.shape[4], points
    )
    weighted = (values * qweight[None, None, :, None, :]).reshape(freq_count, columns, -1)
    flat_values = values.reshape(freq_count, columns, -1)
    gram = jnp.einsum("kcr,kdr->kcd", weighted, flat_values, precision=lax.Precision.HIGHEST)
    local_factor = upper_factor(gram)[None]
    empty = jnp.zeros(gram.shape, jnp.float32)
    summed = add_products(
        empty,
        lax.all_gather(local_factor.astype(jnp.bfloat16), "slab", axis=0, tiled=True).astype(
            jnp.float32
        ),
    )
    factor = upper_factor(summed)
    return (spectra, factor)


def solution(mesh):
    placed = (
        P("slab", None, None, "freq", None, None, None),
        P("slab", None, None),
        P("slab", None),
        P("slab", None, None, None),
        P("slab", None),
    )
    return jax.shard_map(
        body,
        mesh=mesh,
        in_specs=placed,
        out_specs=(P("freq", None, None, "slab", None, None), P("freq", None, None)),
        check_vma=False,
    )
```

profile of v0, /device:TPU:0, one launch (start us, length us, event | category | flops | bytes accessed | tf_op | source)
XLA Modules:
  0.0 303.7 jit_solution(14255040084964306091)
XLA Ops:
  0.6 0.7 bitcast_convert_fusion.2
  1.3 1.4 fusion.54
  3.5 1.0 slice_reduce_fusion.2
  4.5 3.2 %convert_multiply_fusion.2 = (f32[2,8,32,5,256]{4,2,3,1,0:T(8,128)S(1)}, f32[2,8,32,5,256]{4,2,3,1,0:T(8,128)S(1)}, f32[2,8,32,5,256]{4,2,3,1,0:T(8,128)S(1)}) fusion(f32[2,256]{1,0:T(2,128)S(1)} %get-tuple-element.19, bf16[1,3,2,8,32,5,256]{6,4,5,3,2,1,0:T(8,128)(2,1)} %param.6, f32[2,256]{1,0:T(2,128)S(1)} %get-tuple-element.20, ...), kind=kLoop, calls=%fused_computation.12 | loop fusion | flops 3932160 | bytes 11802624 | tf_op jit(solution)/shard_map/mul | solution.py:62
  7.7 5.8 %fusion.9 = f32[2,8,32,5,256]{4,0,3,2,1:T(2,128)S(1)} fusion(f32[2,8,32,5,256]{4,2,3,1,0:T(8,128)S(1)} %get-tuple-element.18, pred[2]{0:T(512)(128)(4,1)S(1)} %iota_compare_fusion.3, s32[2]{0:T(128)S(1)} %get-tuple-element.15), kind=kOutput, calls=%fused_computation.19 | convolution fusion | flops 15728648 | bytes 5242890 | tf_op jit(solution)/shard_map/cq,cbtvp->qbtvp/dot_general | solution.py:63
  13.6 1.3 collective-permute-start
  15.5 5.8 %fusion.7 = f32[2,8,32,5,256]{4,0,3,2,1:T(2,128)S(1)} fusion(f32[2,8,32,5,256]{4,2,3,1,0:T(8,128)S(1)} %get-tuple-element.17, pred[2]{0:T(512)(128)(4,1)S(1)} %iota_compare_fusion.2, s32[2]{0:T(128)S(1)} %get-tuple-element.14), kind=kOutput, calls=%fused_computation.17 | convolution fusion | flops 15728648 | bytes 5242890 | tf_op jit(solution)/shard_map/cq,cbtvp->qbtvp/dot_general | solution.py:63
  21.4 5.7 %collective-permute-start.1 = (f32[2,8,32,5,256]{4,0,3,2,1:T(2,128)S(1)}, f32[2,8,32,5,256]{4,0,3,2,1:T(2,128)S(1)}, u32[]{:S(2)}, u32[]{:S(2)}) collective-permute-start(f32[2,8,32,5,256]{4,0,3,2,1:T(2,128)S(1)} %fusion.7), channel_id=1, source_target_pairs={{0,4},{4,8},{8,12},{12,16},{16,20},{20,24},{24,28},{1,5},{5,9},{9,... | collective-permute-start | bytes 7864328 | tf_op jit(solution)/shard_map/ppermute | solution.py:20
  27.7 47.6 %collective-permute-done = f32[2,8,32,5,256]{4,0,3,2,1:T(2,128)S(1)} collective-permute-done((f32[2,8,32,5,256]{4,0,3,2,1:T(2,128)S(1)}, f32[2,8,32,5,256]{4,0,3,2,1:T(2,128)S(1)}, u32[]{:S(2)}, u32[]{:S(2)}) %collective-permute-start) | collective-permute-done | bytes 2621472 | tf_op jit(solution)/shard_map/ppermute | solution.py:20
  75.3 56.3 %collective-permute-done.1 = f32[2,8,32,5,256]{4,0,3,2,1:T(2,128)S(1)} collective-permute-done((f32[2,8,32,5,256]{4,0,3,2,1:T(2,128)S(1)}, f32[2,8,32,5,256]{4,0,3,2,1:T(2,128)S(1)}, u32[]{:S(2)}, u32[]{:S(2)}) %collective-permute-start.1) | collective-permute-done | bytes 2621472 | tf_op jit(solution)/shard_map/ppermute | solution.py:20
  131.6 7.8 %add_convert_fusion = bf16[2,8,32,5,256]{4,0,3,2,1:T(2,128)(2,1)S(1)} fusion(f32[2,8,32,5,256]{4,0,3,2,1:T(2,128)S(1)} %collective-permute-done.1, f32[2,8,32,5,256]{4,0,3,2,1:T(2,128)S(1)} %collective-permute-done, f32[2,8,32,5,256]{4,2,3,1,0:T(8,128)S(1)} %get-tuple-element.16, pred[2]{0:T(512)(128)(4,1)S(1)} %iota_compare_fusion.4, ...), kind=kOutput, calls=%fused_computation.16 | convolution fusion | flops 17694728 | bytes 9175050 | tf_op jit(solution)/shard_map/cq,cbtvp->qbtvp/dot_general | solution.py:63
  139.4 5.5 %collective-permute-start.2 = (bf16[2,8,32,5,256]{4,0,3,2,1:T(2,128)(2,1)S(1)}, bf16[2,8,32,5,256]{4,0,3,2,1:T(2,128)(2,1)}, u32[]{:S(2)}, u32[]{:S(2)}) collective-permute-start(bf16[2,8,32,5,256]{4,0,3,2,1:T(2,128)(2,1)S(1)} %add_convert_fusion), channel_id=1, source_target_pairs={{0,4},{4,8},{8,12},{12,16},{16,20},{20,24},{24,28},{1,5},{5,9},{9,... | collective-permute-start | bytes 3932168 | tf_op jit(solution)/shard_map/ppermute | solution.py:28
  144.9 1.5 collective-permute-start.3
  146.6 1.0 convert_element_type.143
  149.2 50.9 %collective-permute-done.2 = bf16[2,8,32,5,256]{4,0,3,2,1:T(2,128)(2,1)} collective-permute-done((bf16[2,8,32,5,256]{4,0,3,2,1:T(2,128)(2,1)S(1)}, bf16[2,8,32,5,256]{4,0,3,2,1:T(2,128)(2,1)}, u32[]{:S(2)}, u32[]{:S(2)}) %collective-permute-start.2) | collective-permute-done | bytes 1310752 | tf_op jit(solution)/shard_map/ppermute | solution.py:28
  200.1 5.7 %pad_maximum_fusion = bf16[6,8,32,5,256]{4,0,3,2,1:T(8,128)(2,1)S(1)} fusion(bf16[2,8,32,5,256]{4,0,3,2,1:T(2,128)(2,1)} %collective-permute-done.3, bf16[2,8,32,5,256]{4,0,3,2,1:T(2,128)(2,1)S(1)} %add_convert_fusion, bf16[2,8,32,5,256]{4,0,3,2,1:T(2,128)(2,1)} %collective-permute-done.2), kind=kLoop, calls=%fused_computation | loop fusion | flops 11796480 | bytes 7864320 | tf_op jit(solution)/shard_map/concatenate | solution.py:32
  205.8 4.1 %copy.59 = bf16[6,8,32,5,256]{4,3,2,1,0:T(8,128)(2,1)} copy(bf16[6,8,32,5,256]{4,0,3,2,1:T(8,128)(2,1)S(1)} %pad_maximum_fusion) | data formatting | bytes 7864320 | tf_op jit(solution)/shard_map/concatenate | solution.py:32
  210.0 8.4 %reshape.309 = bf16[7680,256]{1,0:T(8,128)(2,1)} reshape(bf16[6,8,32,5,256]{4,3,2,1,0:T(8,128)(2,1)} %copy.59) | data formatting | bytes 7864320 | tf_op jit(solution)/shard_map/reshape | solution.py:93
  218.4 3.3 %fusion.55 = f32[7680,256]{1,0:T(8,128)S(1)} fusion(bf16[7680,256]{1,0:T(8,128)(2,1)} %reshape.309, bf16[256,256]{1,0:T(8,128)(2,1)S(1)} %convert_element_type.143), kind=kOutput, calls=%fused_computation.93 | convolution fusion | flops 1006632960 | bytes 11927552 | tf_op jit(solution)/shard_map/dot_general | solution.py:93
  221.7 0.8 fusion
  222.5 2.1 reshape.316
  224.7 4.2 %fusion.21 = bf16[8,8,2,2,5,256]{5,0,4,1,3,2:T(8,128)(2,1)S(1)} fusion(f32[2,8,32,5,256]{4,3,2,1,0:T(8,128)} %reshape.316, f32[32,8,1]{0,1,2:T(8,128)S(1)} %get-tuple-element.23, f32[32,8,1]{0,1,2:T(8,128)S(1)} %get-tuple-element.22), kind=kOutput, calls=%fused_computation.28 | convolution fusion | flops 126157312 | bytes 3278848 | tf_op jit(solution)/shard_map/xbtvp,tkr->kbrxvp/dot_general | solution.py:99
  228.9 1.0 copy.61
  229.9 3.7 %all-to-all-start = ((bf16[8,8,2,2,5,256]{5,1,4,3,2,0:T(8,128)(2,1)}), bf16[8,8,2,2,5,256]{5,1,4,3,2,0:T(8,128)(2,1)S(1)}, u32[]{:S(2)}, u32[]{:S(2)}) async-start(bf16[8,8,2,2,5,256]{5,1,4,3,2,0:T(8,128)(2,1)} %copy.61), calls=%async_computation | async-start | bytes 1310720 | tf_op jit(solution)/shard_map/all_to_all | solution.py:102
  233.7 9.9 %all-to-all-done = bf16[8,8,2,2,5,256]{5,1,4,3,2,0:T(8,128)(2,1)S(1)} async-done(((bf16[8,8,2,2,5,256]{5,1,4,3,2,0:T(8,128)(2,1)}), bf16[8,8,2,2,5,256]{5,1,4,3,2,0:T(8,128)(2,1)S(1)}, u32[]{:S(2)}, u32[]{:S(2)}) %all-to-all-start) | async-done | bytes 655392 | tf_op jit(solution)/shard_map/all_to_all | solution.py:102
  243.8 0.7 all_to_all.19
  244.5 0.8 fusion.18
  245.4 11.7 %custom-call.4 = f32[2,64,64]{2,1,0:T(8,128)S(1)} custom-call(f32[2,64,64]{2,1,0:T(8,128)S(1)} %fusion.26), custom_call_target="Cholesky" | custom-call | tf_op jit(solution)/shard_map/jit(cholesky)/cholesky | solution.py:67
  257.5 31.8 %all-gather = bf16[16,64,64]{2,1,0:T(8,128)(2,1)S(1)} all-gather(bf16[2,64,64]{2,1,0:T(8,128)(2,1)S(1)} %copy.65), channel_id=2, replica_groups=mesh['slab'=8,'freq'=4] {'slab'}, dimensions={0}, use_global_device_ids=true | all-gather | bytes 147456 | tf_op jit(solution)/shard_map/all_gather | solution.py:115
  289.7 11.7 %custom-call.5 = f32[2,64,64]{2,1,0:T(8,128)S(1)} custom-call(f32[2,64,64]{2,1,0:T(8,128)S(1)} %fusion.25), custom_call_target="Cholesky" | custom-call | tf_op jit(solution)/shard_map/jit(cholesky)/cholesky | solution.py:67
  301.7 0.7 copy.68
  302.4 1.3 copy.63
  (30 shorter events, 4.4 us)
Async XLA Ops:
  13.6 61.7 %collective-permute-start = (f32[2,8,32,5,256]{4,0,3,2,1:T(2,128)S(1)}, f32[2,8,32,5,256]{4,0,3,2,1:T(2,128)S(1)}, u32[]{:S(2)}, u32[]{:S(2)}) collective-permute-start(f32[2,8,32,5,256]{4,0,3,2,1:T(2,128)S(1)} %fusion.9), channel_id=1, source_target_pairs={{4,0},{8,4},{12,8},{16,12},{20,16},{24,20},{28,24},{5,1},{9,5},{13... | collective-permute-start | bytes 7864328 | tf_op jit(solution)/shard_map/ppermute | solution.py:20
  21.4 110.3 %collective-permute-start.1 = (f32[2,8,32,5,256]{4,0,3,2,1:T(2,128)S(1)}, f32[2,8,32,5,256]{4,0,3,2,1:T(2,128)S(1)}, u32[]{:S(2)}, u32[]{:S(2)}) collective-permute-start(f32[2,8,32,5,256]{4,0,3,2,1:T(2,128)S(1)} %fusion.7), channel_id=1, source_target_pairs={{0,4},{4,8},{8,12},{12,16},{16,20},{20,24},{24,28},{1,5},{5,9},{9,... | collective-permute-start | bytes 7864328 | tf_op jit(solution)/shard_map/ppermute | solution.py:20
  139.4 60.7 %collective-permute-start.2 = (bf16[2,8,32,5,256]{4,0,3,2,1:T(2,128)(2,1)S(1)}, bf16[2,8,32,5,256]{4,0,3,2,1:T(2,128)(2,1)}, u32[]{:S(2)}, u32[]{:S(2)}) collective-permute-start(bf16[2,8,32,5,256]{4,0,3,2,1:T(2,128)(2,1)S(1)} %add_convert_fusion), channel_id=1, source_target_pairs={{0,4},{4,8},{8,12},{12,16},{16,20},{20,24},{24,28},{1,5},{5,9},{9,... | collective-permute-start | bytes 3932168 | tf_op jit(solution)/shard_map/ppermute | solution.py:28
  144.9 55.2 %collective-permute-start.3 = (bf16[2,8,32,5,256]{4,0,3,2,1:T(2,128)(2,1)S(1)}, bf16[2,8,32,5,256]{4,0,3,2,1:T(2,128)(2,1)}, u32[]{:S(2)}, u32[]{:S(2)}) collective-permute-start(bf16[2,8,32,5,256]{4,0,3,2,1:T(2,128)(2,1)S(1)} %add_convert_fusion), channel_id=1, source_target_pairs={{4,0},{8,4},{12,8},{16,12},{20,16},{24,20},{28,24},{5,1},{9,5},{13... | collective-permute-start | bytes 3932168 | tf_op jit(solution)/shard_map/ppermute | solution.py:31
  224.7 8.9 %copy-start = (f32[2,256]{1,0:T(2,128)S(1)}, f32[2,256]{1,0:T(2,128)}, u32[]{:S(2)}) copy-start(f32[2,256]{1,0:T(2,128)} %param.10) | copy-start | bytes 6148
  229.9 13.7 %all-to-all-start = ((bf16[8,8,2,2,5,256]{5,1,4,3,2,0:T(8,128)(2,1)}), bf16[8,8,2,2,5,256]{5,1,4,3,2,0:T(8,128)(2,1)S(1)}, u32[]{:S(2)}, u32[]{:S(2)}) async-start(bf16[8,8,2,2,5,256]{5,1,4,3,2,0:T(8,128)(2,1)} %copy.61), calls=%async_computation | async-start | bytes 1310720 | tf_op jit(solution)/shard_map/all_to_all | solution.py:102
where the time goes:
time: 304 us
  waiting for transfers between devices  165 us (54%)
  other arithmetic  37.6 us (12%)
  blocking collectives  31.8 us (10%)
  matrix products  28 us (9%)
  local copies, waits for them, and re-layouts  22.4 us (7%)
  starting transfers between devices  17.6 us (6%)
    ppermute x2, waiting for transfers between devices, from_behind(): lax.ppermute(value, axis, [(source, source + steps) for source in range(l...  104 us
    ppermute x1, waiting for transfers between devices, padded_2(): lax.ppermute(lax.slice_in_dim(block, block.shape[dim] - width, None, axis...  50.9 us
    all_gather x1, blocking collectives, body(): lax.all_gather(local_factor.astype(jnp.bfloat16), 'slab', axis=0, tiled=T...  31.8 us
    another operation x7, other arithmetic, upper_factor(): return jnp.swapaxes(jnp.linalg.cholesky(gram), 1, 2)  23.8 us
    dot_general x3, matrix products, record_terms(): jnp.einsum('cq,cbtvp->qbtvp', select, scaled, precision=lax.Precision.HIG...  19.4 us
    all_to_all x1, waiting for transfers between devices, body(): lax.all_to_all(local_spec, 'freq', split_axis=0, concat_axis=1, tiled=True)  9.9 us
    reshape x1, local copies, waits for them, and re-layouts, body(): padded.reshape(-1, points)  8.44 us
    ppermute x2, starting transfers between devices, from_behind(): lax.ppermute(value, axis, [(source, source + steps) for source in range(l...  6.96 us
  transfers between devices with their start and end apart: 5, of which 4 were waited for; matrix products, arithmetic and copies ran while one was open for 3% of the time, Pallas kernels for 0%

commit v1 on v0

v1 whole, which is shorter than its diff:
```python
import math

import jax
import jax.numpy as jnp
import numpy as np
from jax import lax
from jax.experimental import pallas as pl
from jax.experimental.pallas import tpu as pltpu
from jax.sharding import PartitionSpec as P

NY = 16
NZ = 16
NF = 8
TAPS = (-0.0625, 0.25, 0.625, 0.25, -0.0625)
BF16 = jnp.bfloat16
F32 = jnp.float32
F16_LOG2 = 14
LOW_LOG2 = -100


def band_matrix(size):
    offset = np.arange(size)[None, :] - np.arange(size)[:, None]
    return sum(TAPS[place] * (offset == place - 2) for place in range(5))


def plane_filter():
    return jnp.asarray(np.kron(band_matrix(NY), band_matrix(NZ)).astype(np.float32), BF16)


def two_parts(value):
    high = value.astype(BF16)
    return high, (value - high.astype(F32)).astype(BF16)


def dft_rows(blocks, times):
    t = np.arange(times)
    window = 0.5 - 0.5 * np.cos(2.0 * math.pi * t / times)
    factor = 1.0 / np.sqrt(np.sum(window * window))
    angle = 2.0 * math.pi * (np.arange(NF)[:, None] + 1.0) * t[None, :] / times
    table = factor * window * np.stack([np.cos(angle), -np.sin(angle)], axis=1)
    rows = np.einsum("krt,bc->kbrct", table, np.eye(blocks))
    rows = rows.reshape(NF * blocks * 2, blocks * times).astype(np.float32)
    high = rows.astype(jnp.bfloat16)
    low = (rows - high.astype(np.float32)).astype(jnp.bfloat16)
    return jnp.asarray(np.concatenate([high, low], axis=0))


def scale_table():
    e = np.arange(128) + LOW_LOG2
    power = np.exp2(e.astype(np.float64))
    factor = np.exp2((F16_LOG2 - e).astype(np.float64))
    rows = np.zeros((8, 128), np.float32)
    rows[0], rows[1], rows[2] = power, factor, e / factor
    return jnp.asarray(rows)


def weight_rows(weight_ref, plane_ref, count_ref, side, plane_total):
    cap = weight_ref.shape[2]
    rows = []
    for q in range(plane_total):
        for c in range(cap):
            live = (plane_ref[0, c, side] == q) & (c < count_ref[0, side])
            row = weight_ref[0, side, c : c + 1, :].astype(F32)
            rows.append(row * jnp.where(live, 1.0, 0.0))
    return rows


def pack_body(plane_total, partials, weight, plane, count, near, far, hold, tail, sems):
    parity = lax.rem(lax.axis_index("slab"), 2)
    pieces = near.shape[0] - 1
    points = near.shape[2]
    loads, stores = [], []
    for place, side in enumerate((1, 2 * parity)):
        load = pltpu.make_async_copy(partials.at[0, side], hold.at[place], sems.at[place])
        load.start()
        loads.append(load)
    for place, (side, target) in enumerate(((1, near), (2 * parity, far))):
        rows = weight_rows(weight, plane, count, side, plane_total)
        filler = jnp.zeros((tail.shape[1] - len(rows), points), F32)
        tail[place] = jnp.concatenate(rows + [filler], axis=0).astype(BF16)
    for place, target in enumerate((near, far)):
        store = pltpu.make_async_copy(tail.at[place], target.at[pieces], sems.at[4 + place])
        store.start()
        stores.append(store)
    for place, target in enumerate((near, far)):
        loads[place].wait()
        store = pltpu.make_async_copy(
            hold.at[place], target.at[pl.ds(0, pieces)], sems.at[2 + place]
        )
        store.start()
        stores.append(store)
    for store in stores:
        store.wait()


def assemble_body(
    dims, partials, weight, plane, count, near, far, dft, kyz, scales, out, factor_out, own, grid, sem
):
    plane_total, cap, blocks, variables, times, points = dims
    parity = lax.rem(lax.axis_index("slab"), 2)
    side = 2 - 2 * parity
    load = pltpu.make_async_copy(partials.at[0, side], own, sem)
    load.start()
    pieces = cap * blocks * variables
    own_rows = weight_rows(weight, plane, count, side, plane_total)
    near_rows = near[pieces].astype(F32)
    far_rows = far[pieces].astype(F32)
    load.wait()
    rows = dft.shape[0] // 2

    def one_variable(v, largest):
        for b in range(blocks):
            totals = [None] * plane_total
            for c in range(cap):
                place = (c * blocks + b) * variables + v
                terms = (own[place], near[place], far[place])
                for at, term in enumerate(terms):
                    value = term.astype(F32)
                    for q in range(plane_total):
                        index = q * cap + c
                        row = (
                            own_rows[index],
                            near_rows[index : index + 1],
                            far_rows[index : index + 1],
                        )[at]
                        product = value * row
                        totals[q] = product if totals[q] is None else totals[q] + product
            for q in range(plane_total):
                grid[q, b * times : (b + 1) * times, :] = totals[q].astype(BF16)
        for q in range(plane_total):
            both = jnp.dot(dft[...], grid[q], preferred_element_type=F32)
            high, low = two_parts(both[:rows] + both[rows:])
            both = jnp.dot(
                jnp.concatenate([high, low], axis=0), kyz[...], preferred_element_type=F32
            )
            coeffs = both[:rows] + both[rows:]
            start = pl.multiple_of((q * variables + v) * rows, rows)
            out[pl.ds(start, rows), :] = coeffs
            for i in range(0, rows, 8):
                largest = jnp.maximum(largest, jnp.abs(coeffs[i : i + 8]))
        return largest

    largest = lax.fori_loop(0, variables, one_variable, jnp.zeros((8, points), F32))
    largest = jnp.max(jnp.max(largest, axis=1, keepdims=True), axis=0, keepdims=True)
    passed = jnp.sum((largest >= scales[0:1, :]).astype(F32), axis=1, keepdims=True)
    lane = lax.broadcasted_iota(jnp.int32, (1, 128), 1).astype(F32)
    hit = lane == passed
    factor = jnp.sum(jnp.where(hit, scales[1:2, :], 0.0), axis=1, keepdims=True)
    mark = jnp.sum(jnp.where(hit, scales[2:3, :], 0.0), axis=1, keepdims=True)
    total = plane_total * variables * rows
    out[total : total + 16, :] = jnp.broadcast_to(mark, (16, points))
    factor_out[...] = jnp.broadcast_to(factor, (8, 128))


def gram_body(values, qweight, out):
    sources, freqs, planes, variables, rows, points = values.shape
    columns = sources * rows
    results = []
    for k in range(freqs):
        total = jnp.zeros((3 * columns, columns), F32)
        for x in range(planes):
            for v in range(variables):
                block = values[:, k, x, v].reshape(columns, points)
                weighted = block.astype(F32) * qweight[x : x + 1, :]
                high, low = two_parts(weighted)
                rest = weighted - high.astype(F32) - low.astype(F32)
                stack = jnp.concatenate([high, low, rest.astype(BF16)], axis=0)
                total = total + lax.dot_general(
                    stack, block, (((1,), (1,)), ((), ())), preferred_element_type=F32
                )
        results.append(total[:columns] + total[columns : 2 * columns] + total[2 * columns :])
    out[...] = jnp.concatenate(results, axis=1)


def factor_body(kept, grams, out):
    columns = grams.shape[1]
    total = jnp.sum(grams[...], axis=0)
    lane = lax.broadcasted_iota(jnp.int32, (8, columns), 1)
    sublane = lax.broadcasted_iota(jnp.int32, (8, columns), 0)
    for start in range(0, columns, 8):
        height = columns - start
        stripes = []
        for t in range(8):
            parts = [
                jnp.broadcast_to(
                    total[:, k * columns + start + t : k * columns + start + t + 1],
                    (height, columns),
                )
                for k in range(kept)
            ]
            stripes.append(jnp.concatenate(parts, axis=1))
        panel = total[:8]
        rows = []
        for t in range(8):
            inverse = lax.rsqrt(stripes[t][t : t + 1])
            stripes[t] = stripes[t] * inverse
            row = panel[t : t + 1] * inverse
            rows.append(row)
            for u in range(t + 1, 8):
                stripes[u] = stripes[u] - stripes[t] * stripes[t][u : u + 1]
            panel = panel - stripes[t][:8] * row
        block = jnp.concatenate(rows, axis=0)
        for k in range(kept):
            piece = block[:, k * columns : (k + 1) * columns]
            out[k, start : start + 8, :] = jnp.where(lane >= sublane + start, piece, 0.0)
        if height > 8:
            total = total[8:]
            for t in range(8):
                total = total - stripes[t][8:] * rows[t]


def pairs(count, even_step, odd_step):
    result = []
    for source in range(count):
        target = source + (odd_step if source % 2 else even_step)
        if 0 <= target < count:
            result.append((source, target))
    return result


def body(partials, rec_plane, rec_count, rec_weight, qweight):
    slabs = lax.axis_size("slab")
    freqs = lax.axis_size("freq")
    plane_total, points = qweight.shape
    _, _, cap, blocks, times, variables, _ = partials.shape
    pieces = cap * blocks * variables
    parity = lax.rem(lax.axis_index("slab"), 2)
    natural = jnp.transpose(partials, (0, 1, 2, 3, 5, 4, 6)).reshape(1, 3, pieces, times, points)
    planes = jnp.swapaxes(rec_plane, 1, 2)
    any_spec = pl.BlockSpec(memory_space=pl.ANY)
    vmem = pl.BlockSpec(memory_space=pltpu.VMEM)
    smem = pl.BlockSpec(memory_space=pltpu.SMEM)

    payload = jax.ShapeDtypeStruct((pieces + 1, times, points), BF16)
    near, far = pl.pallas_call(
        lambda *refs: pack_body(plane_total, *refs),
        out_shape=(payload, payload),
        in_specs=[any_spec, vmem, smem, smem],
        out_specs=(any_spec, any_spec),
        scratch_shapes=[
            pltpu.VMEM((2, pieces, times, points), BF16),
            pltpu.VMEM((2, times, points), BF16),
            pltpu.SemaphoreType.DMA((6,)),
        ],
        name="pack",
    )(natural, rec_weight, planes, rec_count)
    near = lax.ppermute(near, "slab", pairs(slabs, 1, -1))
    far = lax.ppermute(far, "slab", pairs(slabs, -2, 2))

    rows = 2 * NF * blocks
    total = plane_total * variables * rows
    dims = (plane_total, cap, blocks, variables, times, points)
    coeffs, factor = pl.pallas_call(
        lambda *refs: assemble_body(dims, *refs),
        out_shape=(
            jax.ShapeDtypeStruct((total + 16, points), F32),
            jax.ShapeDtypeStruct((8, 128), F32),
        ),
        in_specs=[any_spec, vmem, smem, smem] + [vmem] * 5,
        out_specs=(vmem, vmem),
        scratch_shapes=[
            pltpu.VMEM((pieces, times, points), BF16),
            pltpu.VMEM((plane_total, blocks * times, points), BF16),
            pltpu.SemaphoreType.DMA,
        ],
        name="assemble",
    )(
        natural,
        rec_weight,
        planes,
        rec_count,
        near,
        far,
        dft_rows(blocks, times),
        plane_filter(),
        scale_table(),
    )
    message = (coeffs * factor[0, 0]).astype(jnp.float16)
    middle = lax.ppermute(message, "slab", pairs(slabs, 1, -1))
    beyond = lax.ppermute(message, "slab", pairs(slabs, 2, -2))

    split = (plane_total, variables, NF, 2 * blocks, points)

    def opened(value):
        scale = jnp.exp2(value[total, 0].astype(F32) - F16_LOG2)
        return value[:total].astype(F32).reshape(split) * scale

    own = coeffs[:total].reshape(split)
    mid = opened(middle)
    outer = opened(beyond)
    low = jnp.where(parity == 0, outer, own)
    high = jnp.where(parity == 0, own, outer)
    line = [low[plane_total - 2], low[plane_total - 1]]
    line += [mid[x] for x in range(plane_total)] + [high[0], high[1]]
    local = []
    for x in range(plane_total):
        value = TAPS[0] * line[x]
        for place in range(1, 5):
            value = value + TAPS[place] * line[x + place]
        local.append(jnp.swapaxes(value.astype(BF16), 0, 1))
    local = jnp.stack(local, axis=1)
    values = lax.all_to_all(local, "freq", split_axis=0, concat_axis=0, tiled=True)
    kept = NF // freqs
    values = values.reshape(freqs, kept, plane_total, variables, 2 * blocks, points)
    columns = 2 * blocks * freqs
    gram = pl.pallas_call(
        gram_body,
        out_shape=jax.ShapeDtypeStruct((columns, kept * columns), F32),
        in_specs=[vmem, vmem],
        out_specs=vmem,
        name="gram",
    )(values, qweight)
    spread = jnp.broadcast_to(gram[None], (slabs,) + gram.shape)
    grams = lax.all_to_all(spread, "slab", split_axis=0, concat_axis=0, tiled=True)
    factor = pl.pallas_call(
        lambda *refs: factor_body(kept, *refs),
        out_shape=jax.ShapeDtypeStruct((kept, columns, columns), F32),
        in_specs=[vmem],
        out_specs=vmem,
        name="factor",
    )(grams)
    spectra = values.reshape(freqs, kept, plane_total, variables, blocks, 2, points)
    spectra = jnp.transpose(spectra, (1, 0, 4, 5, 2, 3, 6))
    spectra = spectra.reshape(kept, freqs * blocks, 2, plane_total, variables, points)
    return (spectra, factor)


def solution(mesh):
    placed = (
        P("slab", None, None, "freq", None, None, None),
        P("slab", None, None),
        P("slab", None),
        P("slab", None, None, None),
        P("slab", None),
    )
    return jax.shard_map(
        body,
        mesh=mesh,
        in_specs=placed,
        out_specs=(P("freq", None, None, "slab", None, None), P("freq", None, None)),
        check_vma=False,
    )
```

time: 304 us -> 107 us (0.35)
  waiting for transfers between devices: 165 us -> 52.3 us
  other arithmetic: 37.6 us -> 2.94 us
  matrix products: 28 us -> 0 us
  blocking collectives: 31.8 us -> 13.3 us
  Pallas kernels: 0 us -> 17.2 us
  local copies, waits for them, and re-layouts: 22.4 us -> 7.13 us
  starting transfers between devices: 17.6 us -> 11.8 us
    ppermute x4, waiting for transfers between devices: 155 us -> 45.4 us  [the longest x1 28 us: body(): near = lax.ppermute(near, 'slab', pairs(slabs, 1, -1))]
    all_gather x1 -> x0, blocking collectives: 31.8 us -> none  [body(): lax.all_gather(local_factor.astype(jnp.bfloat16), 'slab', axis=0, tiled=T...]
    dot_general x7 -> x0, matrix products: 28 us -> none  [the longest x3 19.4 us: record_terms(): jnp.einsum('cq,cbtvp->qbtvp', select, scaled, precision=lax.Precision.HIG...]
    another operation x7 -> x1, other arithmetic: 23.8 us -> 0.06 us  [body(): local = jnp.stack(local, axis=1)]
    pallas_call x0 -> x4, Pallas kernels: none -> 17.2 us  [the longest x1 7.62 us: body(): pl.pallas_call(lambda *refs: assemble_body(dims, *refs), out_shape=(jax.S...]
    all_to_all x0 -> x1, blocking collectives: none -> 13.3 us  [body(): lax.all_to_all(local, 'freq', split_axis=0, concat_axis=0, tiled=True)]
    reshape x1 -> x0, local copies, waits for them, and re-layouts: 8.44 us -> none  [body(): padded.reshape(-1, points)]
    ppermute x4, starting transfers between devices: 13.9 us -> 8.04 us  [the longest x1 3.65 us: body(): beyond = lax.ppermute(message, 'slab', pairs(slabs, 2, -2))]
  transfers between devices with their start and end apart: 5 -> 5, of which waited for: 4 -> 5; matrix products, arithmetic and copies ran while one was open for 3% -> 2% of each run, Pallas kernels for 0% -> 0%
where the time goes in v1:
time: 107 us
  waiting for transfers between devices  52.3 us (49%)
  Pallas kernels  17.2 us (16%)
  blocking collectives  13.3 us (12%)
  starting transfers between devices  11.8 us (11%)
  local copies, waits for them, and re-layouts  7.13 us (7%)
  other arithmetic  2.94 us (3%)
  between operations  2.14 us (2%)
    ppermute x1, waiting for transfers between devices, body(): near = lax.ppermute(near, 'slab', pairs(slabs, 1, -1))  28 us
    all_to_all x1, blocking collectives, body(): lax.all_to_all(local, 'freq', split_axis=0, concat_axis=0, tiled=True)  13.3 us
    ppermute x1, waiting for transfers between devices, body(): beyond = lax.ppermute(message, 'slab', pairs(slabs, 2, -2))  12.9 us
    pallas_call x1, Pallas kernels, body(): pl.pallas_call(lambda *refs: assemble_body(dims, *refs), out_shape=(jax.S...  7.62 us
    all_to_all x1, waiting for transfers between devices, body(): lax.all_to_all(spread, 'slab', split_axis=0, concat_axis=0, tiled=True)  6.93 us
    all_to_all x1, starting transfers between devices, body(): lax.all_to_all(spread, 'slab', split_axis=0, concat_axis=0, tiled=True)  3.73 us
    pallas_call x1, Pallas kernels, body(): pl.pallas_call(lambda *refs: pack_body(plane_total, *refs), out_shape=(pa...  3.7 us
    ppermute x1, starting transfers between devices, body(): beyond = lax.ppermute(message, 'slab', pairs(slabs, 2, -2))  3.65 us
  transfers between devices with their start and end apart: 5, of which 5 were waited for; matrix products, arithmetic and copies ran while one was open for 2% of the time, Pallas kernels for 0%

profile of v1, /device:TPU:0, one launch (start us, length us, event | category | flops | bytes accessed | tf_op | source)
XLA Modules:
  0.0 106.8 jit_solution(16052228939509857897)
XLA Ops:
  0.6 3.7 %pack.1 = (bf16[81,32,256]{2,1,0:T(8,128)(2,1)}, bf16[81,32,256]{2,1,0:T(8,128)(2,1)}) custom-call(bf16[1,3,80,32,256]{4,3,2,1,0:T(8,128)(2,1)} %bitcast.23, bf16[1,3,2,256]{3,2,1,0:T(2,128)(2,1)} %refs_1_.3, s32[1,2,3]{2,1,0:T(2,128)} %bitcast.29, s32[1,3]{1,0:T(1,128)} %refs_3_.3), custom_call_target="tpu_custom_call" | custom-call | tf_op jit(solution)/shard_map/pack/pallas_call | solution.py:235
  4.3 3.0 %collective-permute-start = (bf16[81,32,256]{2,1,0:T(8,128)(2,1)}, bf16[81,32,256]{2,1,0:T(8,128)(2,1)S(1)}, u32[]{:S(2)}, u32[]{:S(2)}) collective-permute-start(bf16[81,32,256]{2,1,0:T(8,128)(2,1)} %get-tuple-element.6), channel_id=1, source_target_pairs={{0,4},{4,0},{8,12},{12,8},{16,20},{20,16},{24,28},{28,24},{1,5},{5... | collective-permute-start | bytes 3981320 | tf_op jit(solution)/shard_map/ppermute | solution.py:247
  7.4 1.3 %collective-permute-start.1 = (bf16[81,32,256]{2,1,0:T(8,128)(2,1)}, bf16[81,32,256]{2,1,0:T(8,128)(2,1)S(1)}, u32[]{:S(2)}, u32[]{:S(2)}) collective-permute-start(bf16[81,32,256]{2,1,0:T(8,128)(2,1)} %get-tuple-element.7), channel_id=1, source_target_pairs={{4,12},{8,0},{12,20},{16,8},{20,28},{24,16},{5,13},{9,1},{13,21},{... | collective-permute-start | bytes 3981320 | tf_op jit(solution)/shard_map/ppermute | solution.py:248
  8.7 28.0 %collective-permute-done.refs_4_ = bf16[81,32,256]{2,1,0:T(8,128)(2,1)S(1)} collective-permute-done((bf16[81,32,256]{2,1,0:T(8,128)(2,1)}, bf16[81,32,256]{2,1,0:T(8,128)(2,1)S(1)}, u32[]{:S(2)}, u32[]{:S(2)}) %collective-permute-start) | collective-permute-done | bytes 1327136 | tf_op jit(solution)/shard_map/ppermute | solution.py:247
  36.7 3.3 %collective-permute-done.1.refs_5_ = bf16[81,32,256]{2,1,0:T(8,128)(2,1)S(1)} collective-permute-done((bf16[81,32,256]{2,1,0:T(8,128)(2,1)}, bf16[81,32,256]{2,1,0:T(8,128)(2,1)S(1)}, u32[]{:S(2)}, u32[]{:S(2)}) %collective-permute-start.1) | collective-permute-done | bytes 1327136 | tf_op jit(solution)/shard_map/ppermute | solution.py:248
  40.1 0.0 copy-done.2
  40.1 1.1 %copy-done.3 = bf16[81,32,256]{2,1,0:T(8,128)(2,1)} copy-done((bf16[81,32,256]{2,1,0:T(8,128)(2,1)}, bf16[81,32,256]{2,1,0:T(8,128)(2,1)S(1)}, u32[]{:S(2)}) %copy-start.3) | copy-done | bytes 1327128
  41.1 7.6 %assemble.1 = (f32[1296,256]{1,0:T(8,128)}, f32[8,128]{1,0:T(8,128)}) custom-call(bf16[1,3,80,32,256]{4,3,2,1,0:T(8,128)(2,1)} %bitcast.24, bf16[1,3,2,256]{3,2,1,0:T(2,128)(2,1)} %refs_1_.3, s32[1,2,3]{2,1,0:T(2,128)} %bitcast.30, s32[1,3]{1,0:T(1,128)} %refs_3_.3, bf16[81,32,256]{2,1,0:T(8,128)(2,1)} %copy-done.2, bf16[81,32,256]{2,1,0:T(8,128)(2,1)} %copy-done.3, ...), custom_call_target="tpu_custom_call" | custom-call | tf_op jit(solution)/shard_map/assemble/pallas_call | solution.py:253
  48.8 1.2 %slice.42 = f32[1,1]{1,0:T(1,128)} slice(f32[8,128]{1,0:T(8,128)} %get-tuple-element.9), slice={[0:1], [0:1]} | slice | bytes 8 | tf_op jit(solution)/shard_map/slice | solution.py:278
  50.0 2.1 %multiply_convert_fusion = f16[1296,256]{1,0:T(8,128)(2,1)S(1)} fusion(f32[1296,256]{1,0:T(8,128)} %get-tuple-element.8, f32[]{:T(128)} %bitcast.4), kind=kLoop, calls=%fused_computation | loop fusion | flops 663552 | bytes 1990660 | tf_op jit(solution)/shard_map/convert_element_type | solution.py:278
  52.1 0.0 copy-start.1
  52.1 3.7 %collective-permute-start.2 = (f16[1296,256]{1,0:T(8,128)(2,1)S(1)}, f16[1296,256]{1,0:T(8,128)(2,1)S(1)}, u32[]{:S(2)}, u32[]{:S(2)}) collective-permute-start(f16[1296,256]{1,0:T(8,128)(2,1)S(1)} %multiply_convert_fusion), channel_id=1, source_target_pairs={{0,8},{8,16},{12,4},{16,24},{20,12},{28,20},{1,9},{9,17},{13,5},{1... | collective-permute-start | bytes 1990664 | tf_op jit(solution)/shard_map/ppermute | solution.py:280
  55.8 0.1 collective-permute-start.3
  55.8 12.9 %collective-permute-done.2 = f16[1296,256]{1,0:T(8,128)(2,1)S(1)} collective-permute-done((f16[1296,256]{1,0:T(8,128)(2,1)S(1)}, f16[1296,256]{1,0:T(8,128)(2,1)S(1)}, u32[]{:S(2)}, u32[]{:S(2)}) %collective-permute-start.2) | collective-permute-done | bytes 663584 | tf_op jit(solution)/shard_map/ppermute | solution.py:280
  68.7 0.5 slice.55
  69.9 1.1 %collective-permute-done.3 = f16[1296,256]{1,0:T(8,128)(2,1)S(1)} collective-permute-done((f16[1296,256]{1,0:T(8,128)(2,1)S(1)}, f16[1296,256]{1,0:T(8,128)(2,1)S(1)}, u32[]{:S(2)}, u32[]{:S(2)}) %collective-permute-start.3) | collective-permute-done | bytes 663584 | tf_op jit(solution)/shard_map/ppermute | solution.py:279
  71.1 0.5 slice.59
  72.3 0.1 convert_multiply_fusion
  72.4 0.0 copy-done.1
  72.4 0.2 fusion.1
  72.6 0.4 fusion.8
  73.1 0.1 pad_maximum_fusion
  73.2 13.3 %all_to_all.10 = bf16[8,2,5,16,256]{4,3,2,1,0:T(8,128)(2,1)} all-to-all(bf16[8,2,5,16,256]{4,3,2,1,0:T(8,128)(2,1)S(1)} %pad_maximum_fusion), channel_id=1, replica_groups=mesh['slab'=8,'freq'=4] {'freq'}, dimensions={0} | all-to-all | bytes 1310720 | tf_op jit(solution)/shard_map/all_to_all | solution.py:302
  86.5 2.5 %gram.1 = f32[64,128]{1,0:T(8,128)} custom-call(bf16[4,2,2,5,16,256]{5,4,3,2,1,0:T(8,128)(2,1)} %bitcast.25, f32[2,256]{1,0:T(2,128)} %qweight.1), custom_call_target="tpu_custom_call" | custom-call | tf_op jit(solution)/shard_map/gram/pallas_call | solution.py:306
  89.0 1.5 %broadcast_in_dim.2 = f32[8,64,128]{2,1,0:T(8,128)} broadcast(f32[64,128]{1,0:T(8,128)} %gram.1), dimensions={1,2} | broadcast | bytes 294912 | tf_op jit(solution)/shard_map/broadcast_in_dim | solution.py:313
  90.5 3.7 %all-to-all-start.1 = ((f32[8,64,128]{2,1,0:T(8,128)}), f32[8,64,128]{2,1,0:T(8,128)S(1)}, u32[]{:S(2)}, u32[]{:S(2)}) async-start(f32[8,64,128]{2,1,0:T(8,128)} %broadcast_in_dim.2), calls=%async_computation.1 | async-start | bytes 524288 | tf_op jit(solution)/shard_map/all_to_all | solution.py:314
  94.2 0.0 copy-done
  94.2 0.2 reshape_reshape.3
  94.5 1.4 %copy.12 = bf16[4,2,2,5,8,2,256]{6,2,3,5,4,0,1:T(2,128)(2,1)} copy(bf16[4,2,2,5,8,2,256]{6,5,4,3,2,1,0:T(2,128)(2,1)S(1)} %reshape_reshape.3) | data formatting | bytes 1310720 | tf_op jit(solution)/shard_map/reshape;reshape | solution.py:322
  95.8 6.9 %all-to-all-done.1.refs_0_ = f32[8,64,128]{2,1,0:T(8,128)S(1)} async-done(((f32[8,64,128]{2,1,0:T(8,128)}), f32[8,64,128]{2,1,0:T(8,128)S(1)}, u32[]{:S(2)}, u32[]{:S(2)}) %all-to-all-start.1) | async-done | bytes 262176 | tf_op jit(solution)/shard_map/all_to_all | solution.py:314
  102.8 0.7 copy-done.4
  103.5 3.4 %factor.1 = f32[2,64,64]{2,1,0:T(8,128)} custom-call(f32[8,64,128]{2,1,0:T(8,128)} %copy-done.4), custom_call_target="tpu_custom_call" | custom-call | tf_op jit(solution)/shard_map/factor/pallas_call | solution.py:315
  (5 shorter events, 0.1 us)
Async XLA Ops:
  4.3 32.4 %collective-permute-start = (bf16[81,32,256]{2,1,0:T(8,128)(2,1)}, bf16[81,32,256]{2,1,0:T(8,128)(2,1)S(1)}, u32[]{:S(2)}, u32[]{:S(2)}) collective-permute-start(bf16[81,32,256]{2,1,0:T(8,128)(2,1)} %get-tuple-element.6), channel_id=1, source_target_pairs={{0,4},{4,0},{8,12},{12,8},{16,20},{20,16},{24,28},{28,24},{1,5},{5... | collective-permute-start | bytes 3981320 | tf_op jit(solution)/shard_map/ppermute | solution.py:247
  7.4 32.7 %collective-permute-start.1 = (bf16[81,32,256]{2,1,0:T(8,128)(2,1)}, bf16[81,32,256]{2,1,0:T(8,128)(2,1)S(1)}, u32[]{:S(2)}, u32[]{:S(2)}) collective-permute-start(bf16[81,32,256]{2,1,0:T(8,128)(2,1)} %get-tuple-element.7), channel_id=1, source_target_pairs={{4,12},{8,0},{12,20},{16,8},{20,28},{24,16},{5,13},{9,1},{13,21},{... | collective-permute-start | bytes 3981320 | tf_op jit(solution)/shard_map/ppermute | solution.py:248
  36.7 3.3 %copy-start.2 = (bf16[81,32,256]{2,1,0:T(8,128)(2,1)}, bf16[81,32,256]{2,1,0:T(8,128)(2,1)S(1)}, u32[]{:S(2)}) copy-start(bf16[81,32,256]{2,1,0:T(8,128)(2,1)S(1)} %collective-permute-done.refs_4_) | copy-start | bytes 3981316
  40.1 1.1 %copy-start.3 = (bf16[81,32,256]{2,1,0:T(8,128)(2,1)}, bf16[81,32,256]{2,1,0:T(8,128)(2,1)S(1)}, u32[]{:S(2)}) copy-start(bf16[81,32,256]{2,1,0:T(8,128)(2,1)S(1)} %collective-permute-done.1.refs_5_) | copy-start | bytes 3981316
  52.1 20.3 %copy-start.1 = (f32[1296,256]{1,0:T(8,128)S(1)}, f32[1296,256]{1,0:T(8,128)}, u32[]{:S(2)}) copy-start(f32[1296,256]{1,0:T(8,128)} %get-tuple-element.8) | copy-start | bytes 3981316
  52.1 16.6 %collective-permute-start.2 = (f16[1296,256]{1,0:T(8,128)(2,1)S(1)}, f16[1296,256]{1,0:T(8,128)(2,1)S(1)}, u32[]{:S(2)}, u32[]{:S(2)}) collective-permute-start(f16[1296,256]{1,0:T(8,128)(2,1)S(1)} %multiply_convert_fusion), channel_id=1, source_target_pairs={{0,8},{8,16},{12,4},{16,24},{20,12},{28,20},{1,9},{9,17},{13,5},{1... | collective-permute-start | bytes 1990664 | tf_op jit(solution)/shard_map/ppermute | solution.py:280
  55.8 15.3 %collective-permute-start.3 = (f16[1296,256]{1,0:T(8,128)(2,1)S(1)}, f16[1296,256]{1,0:T(8,128)(2,1)S(1)}, u32[]{:S(2)}, u32[]{:S(2)}) collective-permute-start(f16[1296,256]{1,0:T(8,128)(2,1)S(1)} %multiply_convert_fusion), channel_id=1, source_target_pairs={{0,4},{4,0},{8,12},{12,8},{16,20},{20,16},{24,28},{28,24},{1,5},{5... | collective-permute-start | bytes 1990664 | tf_op jit(solution)/shard_map/ppermute | solution.py:279
  86.5 7.7 %copy-start = (bf16[8,2,5,16,256]{4,3,2,1,0:T(8,128)(2,1)S(1)}, bf16[8,2,5,16,256]{4,3,2,1,0:T(8,128)(2,1)}, u32[]{:S(2)}) copy-start(bf16[8,2,5,16,256]{4,3,2,1,0:T(8,128)(2,1)} %all_to_all.10) | copy-start | bytes 1966084
  90.5 12.3 %all-to-all-start.1 = ((f32[8,64,128]{2,1,0:T(8,128)}), f32[8,64,128]{2,1,0:T(8,128)S(1)}, u32[]{:S(2)}, u32[]{:S(2)}) async-start(f32[8,64,128]{2,1,0:T(8,128)} %broadcast_in_dim.2), calls=%async_computation.1 | async-start | bytes 524288 | tf_op jit(solution)/shard_map/all_to_all | solution.py:314
  102.8 0.7 copy-start.4

commit v2 on v1

v2 whole, which is shorter than its diff:
```python
import math

import jax
import jax.numpy as jnp
import numpy as np
from jax import lax
from jax.experimental import pallas as pl
from jax.experimental.pallas import tpu as pltpu
from jax.sharding import PartitionSpec as P

NY = 16
NZ = 16
NF = 8
TAPS = (-0.0625, 0.25, 0.625, 0.25, -0.0625)
BF16 = jnp.bfloat16
F32 = jnp.float32
F16_LOG2 = 14
LOW_LOG2 = -100
PARAMS = pltpu.CompilerParams(vmem_limit_bytes=24 << 20)


def band_matrix(size):
    offset = np.arange(size)[None, :] - np.arange(size)[:, None]
    return sum(TAPS[place] * (offset == place - 2) for place in range(5))


def plane_filter():
    return jnp.asarray(np.kron(band_matrix(NY), band_matrix(NZ)).astype(np.float32), BF16)


def two_parts(value):
    high = value.astype(BF16)
    return high, (value - high.astype(F32)).astype(BF16)


def dft_rows(blocks, times):
    t = np.arange(times)
    window = 0.5 - 0.5 * np.cos(2.0 * math.pi * t / times)
    factor = 1.0 / np.sqrt(np.sum(window * window))
    angle = 2.0 * math.pi * (np.arange(NF)[:, None] + 1.0) * t[None, :] / times
    table = factor * window * np.stack([np.cos(angle), -np.sin(angle)], axis=1)
    rows = np.einsum("krt,bc->kbrct", table, np.eye(blocks))
    rows = rows.reshape(NF * blocks * 2, blocks * times).astype(np.float32)
    high = rows.astype(jnp.bfloat16)
    low = (rows - high.astype(np.float32)).astype(jnp.bfloat16)
    return jnp.asarray(np.concatenate([high, low], axis=0))


def scale_table():
    e = np.arange(128) + LOW_LOG2
    power = np.exp2(e.astype(np.float64))
    factor = np.exp2((F16_LOG2 - e).astype(np.float64))
    rows = np.zeros((8, 128), np.float32)
    rows[0], rows[1], rows[2] = power, factor, e / factor
    return jnp.asarray(rows)


def weight_rows(weight_ref, plane_ref, count_ref, side, plane_total):
    cap = weight_ref.shape[2]
    rows = []
    for q in range(plane_total):
        for c in range(cap):
            live = (plane_ref[0, c, side] == q) & (c < count_ref[0, side])
            row = weight_ref[0, side, c : c + 1, :].astype(F32)
            rows.append(row * jnp.where(live, 1.0, 0.0))
    return rows


def pack_body(chunk, plane_total, partials, weight, plane, count, near, far, hold, tail, sems):
    first, width = chunk
    parity = lax.rem(lax.axis_index("slab"), 2)
    groups = hold.shape[1]
    sides = (1, 2 * parity)
    loads, stores = [], []
    for place, side in enumerate(sides):
        load = pltpu.make_async_copy(
            partials.at[0, side, :, pl.ds(first, width)], hold.at[place], sems.at[place, groups]
        )
        load.start()
        loads.append(load)
    for place, (side, target) in enumerate(zip(sides, (near, far))):
        rows = weight_rows(weight, plane, count, side, plane_total)
        filler = jnp.zeros((tail.shape[1] - len(rows), tail.shape[2]), F32)
        tail[place] = jnp.concatenate(rows + [filler], axis=0).astype(BF16)
    for place, target in enumerate((near, far)):
        loads[place].wait()
        for g in range(groups):
            store = pltpu.make_async_copy(
                hold.at[place, g], target.at[pl.ds(g * width, width)], sems.at[place, g]
            )
            store.start()
            stores.append(store)
        store = pltpu.make_async_copy(
            tail.at[place], target.at[groups * width], sems.at[place, groups + 1]
        )
        store.start()
        stores.append(store)
    for store in stores:
        store.wait()


def tap_sums(plane_total, start):
    table = []
    for x in range(plane_total):
        places = [start + q - x for q in range(plane_total)]
        table.append([TAPS[at] if 0 <= at < 5 else 0.0 for at in places])
    return table


def assemble_body(
    dims, partials, weight, plane, count, near, far, dft, kyz, scales,
    kept_out, mid_out, outer_out, factor_out, own, near_hold, far_hold, grid, sems,
):
    first, width, plane_total, cap, blocks, times, points = dims
    parity = lax.rem(lax.axis_index("slab"), 2)
    even = parity == 0
    side = 2 - 2 * parity
    loads = [
        pltpu.make_async_copy(
            partials.at[0, side, :, pl.ds(first, width)], own, sems.at[0]
        ),
        pltpu.make_async_copy(near, near_hold, sems.at[1]),
        pltpu.make_async_copy(far, far_hold, sems.at[2]),
    ]
    for load in loads:
        load.start()
    pieces = cap * blocks * width
    own_rows = weight_rows(weight, plane, count, side, plane_total)
    for load in loads:
        load.wait()
    near_rows = near_hold[pieces].astype(F32)
    far_rows = far_hold[pieces].astype(F32)
    rows = dft.shape[0] // 2
    height = 2 * blocks
    low = tap_sums(plane_total, 2 - plane_total)
    mid = tap_sums(plane_total, 2)
    high = tap_sums(plane_total, 2 + plane_total)
    largest = jnp.zeros((8, points), F32)
    for v in range(width):
        for b in range(blocks):
            totals = [None] * plane_total
            for c in range(cap):
                group = c * blocks + b
                terms = (own[group, v], near_hold[group * width + v], far_hold[group * width + v])
                for at, term in enumerate(terms):
                    value = term.astype(F32)
                    for q in range(plane_total):
                        index = q * cap + c
                        row = (
                            own_rows[index],
                            near_rows[index : index + 1],
                            far_rows[index : index + 1],
                        )[at]
                        product = value * row
                        totals[q] = product if totals[q] is None else totals[q] + product
            for q in range(plane_total):
                grid[q, b * times : (b + 1) * times, :] = totals[q].astype(BF16)
        coeffs = []
        for q in range(plane_total):
            both = jnp.dot(dft[...], grid[q], preferred_element_type=F32)
            high_part, low_part = two_parts(both[:rows] + both[rows:])
            both = jnp.dot(
                jnp.concatenate([high_part, low_part], axis=0),
                kyz[...],
                preferred_element_type=F32,
            )
            coeffs.append(both[:rows] + both[rows:])
        for x in range(plane_total):
            kept = sent = middle = 0.0
            for q in range(plane_total):
                lower, upper = low[x][q], high[x][q]
                kept = kept + coeffs[q] * jnp.where(even, upper, lower)
                sent = sent + coeffs[q] * jnp.where(even, lower, upper)
                middle = middle + coeffs[q] * mid[x][q]
            for i in range(0, rows, 8):
                part = jnp.maximum(jnp.abs(sent[i : i + 8]), jnp.abs(middle[i : i + 8]))
                largest = jnp.maximum(largest, part)
            for k in range(rows // height):
                start = ((k * plane_total + x) * width + v) * height
                for target, value in ((kept_out, kept), (mid_out, middle), (outer_out, sent)):
                    target[start : start + height, :] = value[k * height : (k + 1) * height]
    largest = jnp.max(jnp.max(largest, axis=1, keepdims=True), axis=0, keepdims=True)
    passed = jnp.sum((largest >= scales[0:1, :]).astype(F32), axis=1, keepdims=True)
    lane = lax.broadcasted_iota(jnp.int32, (1, 128), 1).astype(F32)
    hit = lane == passed
    factor = jnp.sum(jnp.where(hit, scales[1:2, :], 0.0), axis=1, keepdims=True)
    mark = jnp.sum(jnp.where(hit, scales[2:3, :], 0.0), axis=1, keepdims=True)
    total = plane_total * width * rows
    for target in (mid_out, outer_out):
        target[total : total + 16, :] = jnp.broadcast_to(mark, (16, points))
    factor_out[...] = jnp.broadcast_to(factor, (8, 128))


def gram_body(values, qweight, *refs):
    *before, out = refs
    sources, freqs, planes, variables, rows, points = values.shape
    columns = sources * rows
    results = []
    for k in range(freqs):
        total = jnp.zeros((3 * columns, columns), F32)
        for x in range(planes):
            for v in range(variables):
                block = values[:, k, x, v].reshape(columns, points)
                weighted = block.astype(F32) * qweight[x : x + 1, :]
                high, low = two_parts(weighted)
                rest = weighted - high.astype(F32) - low.astype(F32)
                stack = jnp.concatenate([high, low, rest.astype(BF16)], axis=0)
                total = total + lax.dot_general(
                    stack, block, (((1,), (1,)), ((), ())), preferred_element_type=F32
                )
        results.append(total[:columns] + total[columns : 2 * columns] + total[2 * columns :])
    result = jnp.concatenate(results, axis=1)
    for earlier in before:
        result = result + earlier[0]
    for copy in range(out.shape[0]):
        out[copy] = result


def factor_body(kept, grams, out):
    columns = grams.shape[1]
    total = jnp.sum(grams[...], axis=0)
    lane = lax.broadcasted_iota(jnp.int32, (8, columns), 1)
    sublane = lax.broadcasted_iota(jnp.int32, (8, columns), 0)
    for start in range(0, columns, 8):
        height = columns - start
        stripes = []
        for t in range(8):
            parts = [
                jnp.broadcast_to(
                    total[:, k * columns + start + t : k * columns + start + t + 1],
                    (height, columns),
                )
                for k in range(kept)
            ]
            stripes.append(jnp.concatenate(parts, axis=1))
        panel = total[:8]
        rows = []
        for t in range(8):
            inverse = lax.rsqrt(stripes[t][t : t + 1])
            stripes[t] = stripes[t] * inverse
            row = panel[t : t + 1] * inverse
            rows.append(row)
            for u in range(t + 1, 8):
                stripes[u] = stripes[u] - stripes[t] * stripes[t][u : u + 1]
            panel = panel - stripes[t][:8] * row
        block = jnp.concatenate(rows, axis=0)
        for k in range(kept):
            piece = block[:, k * columns : (k + 1) * columns]
            out[k, start : start + 8, :] = jnp.where(lane >= sublane + start, piece, 0.0)
        if height > 8:
            total = total[8:]
            for t in range(8):
                total = total - stripes[t][8:] * rows[t]


def pairs(count, even_step, odd_step):
    result = []
    for source in range(count):
        target = source + (odd_step if source % 2 else even_step)
        if 0 <= target < count:
            result.append((source, target))
    return result


def chunks_of(variables):
    head = (3 * variables + 2) // 5
    return [(0, head), (head, variables - head)] if head < variables else [(0, variables)]


def body(partials, rec_plane, rec_count, rec_weight, qweight):
    slabs = lax.axis_size("slab")
    freqs = lax.axis_size("freq")
    plane_total, points = qweight.shape
    _, _, cap, blocks, times, variables, _ = partials.shape
    groups = cap * blocks
    natural = jnp.transpose(partials, (0, 1, 2, 3, 5, 4, 6))
    natural = natural.reshape(1, 3, groups, variables, times, points)
    natural = pltpu.with_memory_space_constraint(natural, pltpu.HBM)
    planes = jnp.swapaxes(rec_plane, 1, 2)
    any_spec = pl.BlockSpec(memory_space=pl.ANY)
    hbm = pl.BlockSpec(memory_space=pltpu.HBM)
    vmem = pl.BlockSpec(memory_space=pltpu.VMEM)
    smem = pl.BlockSpec(memory_space=pltpu.SMEM)
    dft, kyz, scales = dft_rows(blocks, times), plane_filter(), scale_table()
    kept = NF // freqs
    height = 2 * blocks
    columns = height * freqs
    chunks = chunks_of(variables)

    def raw(chunk, weight):
        width = chunk[1]
        payload = jax.ShapeDtypeStruct((groups * width + 1, times, points), BF16)
        near, far = pl.pallas_call(
            lambda *refs: pack_body(chunk, plane_total, *refs),
            out_shape=(payload, payload),
            in_specs=[hbm, vmem, smem, smem],
            out_specs=(any_spec, any_spec),
            scratch_shapes=[
                pltpu.VMEM((2, groups, width, times, points), BF16),
                pltpu.VMEM((2, times, points), BF16),
                pltpu.SemaphoreType.DMA((2, groups + 2)),
            ],
            name="pack",
        )(natural, weight, planes, rec_count)
        weight, near, far = lax.optimization_barrier((weight, near, far))
        near = lax.ppermute(near, "slab", pairs(slabs, 1, -1))
        far = lax.ppermute(far, "slab", pairs(slabs, -2, 2))
        return weight, (near, far)

    def assembled(chunk, weight, near, far):
        width = chunk[1]
        total = NF * plane_total * width * height
        dims = chunk + (plane_total, cap, blocks, times, points)
        own, middle, outer, factor = pl.pallas_call(
            lambda *refs: assemble_body(dims, *refs),
            out_shape=(
                jax.ShapeDtypeStruct((total, points), F32),
                jax.ShapeDtypeStruct((total + 16, points), F32),
                jax.ShapeDtypeStruct((total + 16, points), F32),
                jax.ShapeDtypeStruct((8, 128), F32),
            ),
            in_specs=[hbm, vmem, smem, smem, any_spec, any_spec] + [vmem] * 3,
            out_specs=(vmem,) * 4,
            scratch_shapes=[
                pltpu.VMEM((groups, width, times, points), BF16),
                pltpu.VMEM((groups * width + 1, times, points), BF16),
                pltpu.VMEM((groups * width + 1, times, points), BF16),
                pltpu.VMEM((plane_total, blocks * times, points), BF16),
                pltpu.SemaphoreType.DMA((3,)),
            ],
            compiler_params=PARAMS,
            name="assemble",
        )(natural, weight, planes, rec_count, near, far, dft, kyz, scales)
        middle, outer = (
            (value * factor[0, 0]).astype(jnp.float16) for value in (middle, outer)
        )
        weight, own, middle, outer = lax.optimization_barrier((weight, own, middle, outer))
        middle = lax.ppermute(middle, "slab", pairs(slabs, 1, -1))
        outer = lax.ppermute(outer, "slab", pairs(slabs, 2, -2))
        return weight, (own, middle, outer)

    def combined(chunk, token, own, middle, outer):
        width = chunk[1]
        total = own.shape[0]
        own, middle, outer, token = lax.optimization_barrier((own, middle, outer, token))
        for message in (middle, outer):
            scale = jnp.exp2(message[total : total + 1].astype(F32) - F16_LOG2)
            own = own + message[:total].astype(F32) * scale
        own = own.astype(BF16)
        local = own.reshape(NF, plane_total, width, height, points)
        values = lax.all_to_all(local, "freq", split_axis=0, concat_axis=0, tiled=True)
        return own, values.reshape(freqs, kept, plane_total, width, height, points)

    def partial_gram(values, before, copies):
        return pl.pallas_call(
            gram_body,
            out_shape=jax.ShapeDtypeStruct((copies, columns, kept * columns), F32),
            in_specs=[vmem] * (2 + len(before)),
            out_specs=vmem,
            compiler_params=PARAMS,
            name="gram",
        )(values, qweight, *before)

    arrived = []
    weight = rec_weight
    for chunk in chunks:
        weight, records = raw(chunk, weight)
        arrived.append(records)
    sent = []
    for chunk, records in zip(chunks, arrived):
        weight, parts = assembled(chunk, weight, *records)
        sent.append(parts)
    values = []
    token = qweight
    for chunk, parts in zip(chunks, sent):
        token, value = combined(chunk, token, *parts)
        values.append(value)
    gram = ()
    for at, value in enumerate(values):
        copies = slabs if at == len(values) - 1 else 1
        gram = (partial_gram(value, gram, copies),)
    grams = lax.all_to_all(gram[0], "slab", split_axis=0, concat_axis=0, tiled=True)
    factor = pl.pallas_call(
        lambda *refs: factor_body(kept, *refs),
        out_shape=jax.ShapeDtypeStruct((kept, columns, columns), F32),
        in_specs=[vmem],
        out_specs=vmem,
        compiler_params=PARAMS,
        name="factor",
    )(grams)
    spectra = jnp.concatenate(values, axis=3)
    spectra = spectra.reshape(freqs, kept, plane_total, variables, blocks, 2, points)
    spectra = jnp.transpose(spectra, (1, 0, 4, 5, 2, 3, 6))
    spectra = spectra.reshape(kept, freqs * blocks, 2, plane_total, variables, points)
    return (spectra, factor)


def solution(mesh):
    placed = (
        P("slab", None, None, "freq", None, None, None),
        P("slab", None, None),
        P("slab", None),
        P("slab", None, None, None),
        P("slab", None),
    )
    return jax.shard_map(
        body,
        mesh=mesh,
        in_specs=placed,
        out_specs=(P("freq", None, None, "slab", None, None), P("freq", None, None)),
        check_vma=False,
    )
```

time: 107 us -> 87.9 us (0.82)
  waiting for transfers between devices: 52.3 us -> 33.7 us
  starting transfers between devices: 11.8 us -> 28.1 us
  blocking collectives: 13.3 us -> 0 us
  local copies, waits for them, and re-layouts: 7.13 us -> 1.91 us
  other arithmetic: 2.94 us -> 5.74 us
  between operations: 2.14 us -> 0.94 us
    ppermute x4 -> x8, waiting for transfers between devices: 45.4 us -> 15.7 us  [the longest x2 10.4 us: raw(): near = lax.ppermute(near, 'slab', pairs(slabs, 1, -1))]
    all_to_all x1 -> x0, blocking collectives: 13.3 us -> none  [body(): lax.all_to_all(local, 'freq', split_axis=0, concat_axis=0, tiled=True)]
    all_to_all x1 -> x3, waiting for transfers between devices: 6.93 us -> 18 us  [the longest x2 11.9 us: combined(): lax.all_to_all(local, 'freq', split_axis=0, concat_axis=0, tiled=True)]
    ppermute x4 -> x8, starting transfers between devices: 8.04 us -> 16.6 us  [the longest x2 8.02 us: assembled(): outer = lax.ppermute(outer, 'slab', pairs(slabs, 2, -2))]
    all_to_all x1 -> x3, starting transfers between devices: 3.73 us -> 11.5 us  [the longest x2 6.86 us: combined(): lax.all_to_all(local, 'freq', split_axis=0, concat_axis=0, tiled=True)]
    unnamed x10 -> x14, local copies, waits for them, and re-layouts: 1.79 us -> 0.05 us
    concatenate x0 -> x1, other arithmetic: none -> 1.68 us  [body(): spectra = jnp.concatenate(values, axis=3)]
    another operation x3 -> x0, local copies, waits for them, and re-layouts: 1.65 us -> none  [the longest x2 1.6 us: body(): values.reshape(freqs, kept, plane_total, variables, blocks, 2, points)]
  transfers between devices with their start and end apart: 5 -> 11, of which waited for: 5 -> 6; matrix products, arithmetic and copies ran while one was open for 2% -> 9% of each run, Pallas kernels for 0% -> 11%
where the time goes in v2:
time: 87.9 us; the launch traced here: 87.2 us
  waiting for transfers between devices  33.7 us (38%)
  starting transfers between devices  28.1 us (32%)
  Pallas kernels  16.8 us (19%)
  other arithmetic  5.74 us (7%)
  local copies, waits for them, and re-layouts  1.91 us (2%)
  between operations  0.94 us (1%)
    all_to_all x2, waiting for transfers between devices, combined(): lax.all_to_all(local, 'freq', split_axis=0, concat_axis=0, tiled=True)  11.9 us
    ppermute x2, waiting for transfers between devices, raw(): near = lax.ppermute(near, 'slab', pairs(slabs, 1, -1))  10.4 us
    ppermute x2, starting transfers between devices, assembled(): outer = lax.ppermute(outer, 'slab', pairs(slabs, 2, -2))  8.02 us
    all_to_all x2, starting transfers between devices, combined(): lax.all_to_all(local, 'freq', split_axis=0, concat_axis=0, tiled=True)  6.86 us
    pallas_call x2, Pallas kernels, raw(): pl.pallas_call(lambda *refs: pack_body(chunk, plane_total, *refs), out_sh...  6.6 us
    pallas_call x2, Pallas kernels, assembled(): pl.pallas_call(lambda *refs: assemble_body(dims, *refs), out_shape=(jax.S...  6.1 us
    all_to_all x1, waiting for transfers between devices, body(): lax.all_to_all(gram[0], 'slab', split_axis=0, concat_axis=0, tiled=True)  6.07 us
    ppermute x2, starting transfers between devices, raw(): near = lax.ppermute(near, 'slab', pairs(slabs, 1, -1))  5.87 us
  transfers between devices with their start and end apart: 11, of which 6 were waited for; matrix products, arithmetic and copies ran while one was open for 9% of the time, Pallas kernels for 11%

profile of v2, /device:TPU:0, one launch (start us, length us, event | category | flops | bytes accessed | tf_op | source)
XLA Modules:
  0.0 87.2 jit_solution(16893210580146943884)
XLA Ops:
  0.7 3.5 %pack.2 = (bf16[49,32,256]{2,1,0:T(8,128)(2,1)}, bf16[49,32,256]{2,1,0:T(8,128)(2,1)}) custom-call(bf16[1,3,16,5,32,256]{5,4,3,2,1,0:T(8,128)(2,1)} %bitcast.27, bf16[1,3,2,256]{3,2,1,0:T(2,128)(2,1)} %refs_1_.4, s32[1,2,3]{2,1,0:T(2,128)} %bitcast.23, s32[1,3]{1,0:T(1,128)} %refs_3_.7), custom_call_target="tpu_custom_call" | custom-call | tf_op jit(solution)/shard_map/pack/pallas_call | solution.py:293
  4.2 3.0 %collective-permute-start = (bf16[49,32,256]{2,1,0:T(8,128)(2,1)}, bf16[49,32,256]{2,1,0:T(8,128)(2,1)S(1)}, u32[]{:S(2)}, u32[]{:S(2)}) collective-permute-start(bf16[49,32,256]{2,1,0:T(8,128)(2,1)} %get-tuple-element.39), channel_id=1, source_target_pairs={{0,4},{4,0},{8,12},{12,8},{16,20},{20,16},{24,28},{28,24},{1,5},{5... | collective-permute-start | bytes 2408456 | tf_op jit(solution)/shard_map/ppermute | solution.py:306
  7.2 1.3 %collective-permute-start.1 = (bf16[49,32,256]{2,1,0:T(8,128)(2,1)}, bf16[49,32,256]{2,1,0:T(8,128)(2,1)S(1)}, u32[]{:S(2)}, u32[]{:S(2)}) collective-permute-start(bf16[49,32,256]{2,1,0:T(8,128)(2,1)} %get-tuple-element.40), channel_id=1, source_target_pairs={{4,12},{8,0},{12,20},{16,8},{20,28},{24,16},{5,13},{9,1},{13,21},{... | collective-permute-start | bytes 2408456 | tf_op jit(solution)/shard_map/ppermute | solution.py:307
  8.5 3.1 %pack.3 = (bf16[33,32,256]{2,1,0:T(8,128)(2,1)}, bf16[33,32,256]{2,1,0:T(8,128)(2,1)}) custom-call(bf16[1,3,16,5,32,256]{5,4,3,2,1,0:T(8,128)(2,1)} %bitcast.28, bf16[1,3,2,256]{3,2,1,0:T(2,128)(2,1)} %refs_1_.4, s32[1,2,3]{2,1,0:T(2,128)} %bitcast.24, s32[1,3]{1,0:T(1,128)} %refs_3_.7), custom_call_target="tpu_custom_call" | custom-call | tf_op jit(solution)/shard_map/pack/pallas_call | solution.py:293
  11.6 2.8 %collective-permute-start.4 = (bf16[33,32,256]{2,1,0:T(8,128)(2,1)}, bf16[33,32,256]{2,1,0:T(8,128)(2,1)S(1)}, u32[]{:S(2)}, u32[]{:S(2)}) collective-permute-start(bf16[33,32,256]{2,1,0:T(8,128)(2,1)} %get-tuple-element.52), channel_id=1, source_target_pairs={{0,4},{4,0},{8,12},{12,8},{16,20},{20,16},{24,28},{28,24},{1,5},{5... | collective-permute-start | bytes 1622024 | tf_op jit(solution)/shard_map/ppermute | solution.py:306
  14.5 1.3 %collective-permute-start.5 = (bf16[33,32,256]{2,1,0:T(8,128)(2,1)}, bf16[33,32,256]{2,1,0:T(8,128)(2,1)S(1)}, u32[]{:S(2)}, u32[]{:S(2)}) collective-permute-start(bf16[33,32,256]{2,1,0:T(8,128)(2,1)} %get-tuple-element.53), channel_id=1, source_target_pairs={{4,12},{8,0},{12,20},{16,8},{20,28},{24,16},{5,13},{9,1},{13,21},{... | collective-permute-start | bytes 1622024 | tf_op jit(solution)/shard_map/ppermute | solution.py:307
  15.8 10.4 %collective-permute-done.refs_4_ = bf16[49,32,256]{2,1,0:T(8,128)(2,1)S(1)} collective-permute-done((bf16[49,32,256]{2,1,0:T(8,128)(2,1)}, bf16[49,32,256]{2,1,0:T(8,128)(2,1)S(1)}, u32[]{:S(2)}, u32[]{:S(2)}) %collective-permute-start) | collective-permute-done | bytes 802848 | tf_op jit(solution)/shard_map/ppermute | solution.py:306
  26.2 3.9 %collective-permute-done.1.refs_5_ = bf16[49,32,256]{2,1,0:T(8,128)(2,1)S(1)} collective-permute-done((bf16[49,32,256]{2,1,0:T(8,128)(2,1)}, bf16[49,32,256]{2,1,0:T(8,128)(2,1)S(1)}, u32[]{:S(2)}, u32[]{:S(2)}) %collective-permute-start.1) | collective-permute-done | bytes 802848 | tf_op jit(solution)/shard_map/ppermute | solution.py:307
  30.1 3.3 %assemble.2 = (f32[768,256]{1,0:T(8,128)S(1)}, f32[784,256]{1,0:T(8,128)S(1)}, f32[784,256]{1,0:T(8,128)S(1)}, f32[8,128]{1,0:T(8,128)S(1)}) custom-call(bf16[1,3,16,5,32,256]{5,4,3,2,1,0:T(8,128)(2,1)} %bitcast.29, bf16[1,3,2,256]{3,2,1,0:T(2,128)(2,1)S(1)} %copy-done.2, s32[1,2,3]{2,1,0:T(2,128)S(1)} %bitcast.25, s32[1,3]{1,0:T(1,128)S(1)} %copy-done.6, ...), custom_call_target="tpu_custom_call" | custom-call | tf_op jit(solution)/shard_map/assemble/pallas_call | solution.py:314
  33.4 0.5 slice.32
  33.9 0.8 multiply_convert_fusion
  34.8 4.0 %collective-permute-start.3 = (f16[784,256]{1,0:T(8,128)(2,1)S(1)}, f16[784,256]{1,0:T(8,128)(2,1)S(1)}, u32[]{:S(2)}, u32[]{:S(2)}) collective-permute-start(f16[784,256]{1,0:T(8,128)(2,1)S(1)} %get-tuple-element.47), channel_id=1, source_target_pairs={{0,8},{8,16},{12,4},{16,24},{20,12},{28,20},{1,9},{9,17},{13,5},{1... | collective-permute-start | bytes 1204232 | tf_op jit(solution)/shard_map/ppermute | solution.py:339
  38.8 1.4 %collective-permute-done.5.refs_5_ = bf16[33,32,256]{2,1,0:T(8,128)(2,1)S(1)} collective-permute-done((bf16[33,32,256]{2,1,0:T(8,128)(2,1)}, bf16[33,32,256]{2,1,0:T(8,128)(2,1)S(1)}, u32[]{:S(2)}, u32[]{:S(2)}) %collective-permute-start.5) | collective-permute-done | bytes 540704 | tf_op jit(solution)/shard_map/ppermute | solution.py:307
  40.2 2.8 %assemble.3 = (f32[512,256]{1,0:T(8,128)S(1)}, f32[528,256]{1,0:T(8,128)S(1)}, f32[528,256]{1,0:T(8,128)S(1)}, f32[8,128]{1,0:T(8,128)S(1)}) custom-call(bf16[1,3,16,5,32,256]{5,4,3,2,1,0:T(8,128)(2,1)} %bitcast.30, bf16[1,3,2,256]{3,2,1,0:T(2,128)(2,1)S(1)} %copy-done.2, s32[1,2,3]{2,1,0:T(2,128)S(1)} %bitcast.26, s32[1,3]{1,0:T(1,128)S(1)} %copy-done.6, ...), custom_call_target="tpu_custom_call" | custom-call | tf_op jit(solution)/shard_map/assemble/pallas_call | solution.py:314
  43.1 0.5 slice.37
  43.6 0.7 multiply_convert_fusion.3
  44.3 0.7 multiply_convert_fusion.2
  45.1 4.0 %collective-permute-start.7 = (f16[528,256]{1,0:T(8,128)(2,1)S(1)}, f16[528,256]{1,0:T(8,128)(2,1)S(1)}, u32[]{:S(2)}, u32[]{:S(2)}) collective-permute-start(f16[528,256]{1,0:T(8,128)(2,1)S(1)} %multiply_convert_fusion.2), channel_id=1, source_target_pairs={{0,8},{8,16},{12,4},{16,24},{20,12},{28,20},{1,9},{9,17},{13,5},{1... | collective-permute-start | bytes 811016 | tf_op jit(solution)/shard_map/ppermute | solution.py:339
  49.2 1.0 %add_convert_fusion = bf16[768,256]{1,0:T(8,128)(2,1)} fusion(f32[768,256]{1,0:T(8,128)S(1)} %get-tuple-element.48, f32[256]{0:T(256)S(1)} %bitcast.33, f16[784,256]{1,0:T(8,128)(2,1)S(1)} %collective-permute-done.3, f32[256]{0:T(256)S(1)} %bitcast.32, f16[784,256]{1,0:T(8,128)(2,1)S(1)} %collective-permute-done.2), kind=kLoop, calls=%fused_computation.2 | loop fusion | flops 1376256 | bytes 1968128 | tf_op jit(solution)/shard_map/convert_element_type | solution.py:349
  50.1 3.5 %all-to-all-start = ((bf16[8,2,3,16,256]{4,3,2,1,0:T(8,128)(2,1)}), bf16[8,2,3,16,256]{4,3,2,1,0:T(8,128)(2,1)S(1)}, u32[]{:S(2)}, u32[]{:S(2)}) async-start(bf16[8,2,3,16,256]{4,3,2,1,0:T(8,128)(2,1)} %bitcast.7), calls=%async_computation | async-start | bytes 786432 | tf_op jit(solution)/shard_map/all_to_all | solution.py:351
  53.6 0.8 add_convert_fusion.1
  54.5 6.5 %all-to-all-done = bf16[8,2,3,16,256]{4,3,2,1,0:T(8,128)(2,1)S(1)} async-done(((bf16[8,2,3,16,256]{4,3,2,1,0:T(8,128)(2,1)}), bf16[8,2,3,16,256]{4,3,2,1,0:T(8,128)(2,1)S(1)}, u32[]{:S(2)}, u32[]{:S(2)}) %all-to-all-start) | async-done | bytes 393248 | tf_op jit(solution)/shard_map/all_to_all | solution.py:351
  61.0 3.4 %all-to-all-start.1 = ((bf16[8,2,2,16,256]{4,3,2,1,0:T(8,128)(2,1)}), bf16[8,2,2,16,256]{4,3,2,1,0:T(8,128)(2,1)S(1)}, u32[]{:S(2)}, u32[]{:S(2)}) async-start(bf16[8,2,2,16,256]{4,3,2,1,0:T(8,128)(2,1)} %bitcast.11), calls=%async_computation.1 | async-start | bytes 524288 | tf_op jit(solution)/shard_map/all_to_all | solution.py:351
  64.4 0.5 gram.2.refs_0_
  64.9 5.4 %all-to-all-done.1 = bf16[8,2,2,16,256]{4,3,2,1,0:T(8,128)(2,1)S(1)} async-done(((bf16[8,2,2,16,256]{4,3,2,1,0:T(8,128)(2,1)}), bf16[8,2,2,16,256]{4,3,2,1,0:T(8,128)(2,1)S(1)}, u32[]{:S(2)}, u32[]{:S(2)}) %all-to-all-start.1) | async-done | bytes 262176 | tf_op jit(solution)/shard_map/all_to_all | solution.py:351
  70.3 1.1 %gram.3 = f32[8,64,128]{2,1,0:T(8,128)} custom-call(bf16[4,2,2,2,16,256]{5,4,3,2,1,0:T(8,128)(2,1)S(1)} %bitcast.22, f32[2,256]{1,0:T(2,128)S(1)} %copy-done.5, f32[1,64,128]{2,1,0:T(8,128)S(1)} %gram.2.refs_0_), custom_call_target="tpu_custom_call" | custom-call | tf_op jit(solution)/shard_map/gram/pallas_call | solution.py:355
  71.5 4.7 %all-to-all-start.2 = ((f32[8,64,128]{2,1,0:T(8,128)}), f32[8,64,128]{2,1,0:T(8,128)S(1)}, u32[]{:S(2)}, u32[]{:S(2)}) async-start(f32[8,64,128]{2,1,0:T(8,128)} %gram.3), calls=%async_computation.2 | async-start | bytes 524288 | tf_op jit(solution)/shard_map/all_to_all | solution.py:382
  76.3 0.3 copy.11
  76.7 0.3 copy.10
  77.0 1.7 %pad_maximum_fusion = bf16[4,2,2,5,8,2,256]{6,2,3,5,4,0,1:T(2,128)(2,1)} fusion(bf16[4,2,2,2,8,2,256]{6,2,3,5,4,0,1:T(2,128)(2,1)S(1)} %copy.11, bf16[4,2,2,3,8,2,256]{6,2,3,5,4,0,1:T(2,128)(2,1)S(1)} %copy.10), kind=kLoop, calls=%fused_computation.3 | loop fusion | flops 327680 | bytes 1310720 | tf_op jit(solution)/shard_map/concatenate | solution.py:391
  78.7 6.1 %all-to-all-done.2.refs_0_ = f32[8,64,128]{2,1,0:T(8,128)S(1)} async-done(((f32[8,64,128]{2,1,0:T(8,128)}), f32[8,64,128]{2,1,0:T(8,128)S(1)}, u32[]{:S(2)}, u32[]{:S(2)}) %all-to-all-start.2) | async-done | bytes 262176 | tf_op jit(solution)/shard_map/all_to_all | solution.py:382
  84.8 2.5 %factor.1 = f32[2,64,64]{2,1,0:T(8,128)} custom-call(f32[8,64,128]{2,1,0:T(8,128)S(1)} %all-to-all-done.2.refs_0_), custom_call_target="tpu_custom_call" | custom-call | tf_op jit(solution)/shard_map/factor/pallas_call | solution.py:383
  (27 shorter events, 0.5 us)
Async XLA Ops:
  0.6 29.4 %copy-start = (bf16[256,256]{1,0:T(8,128)(2,1)S(1)}, bf16[256,256]{1,0:T(8,128)(2,1)}, u32[]{:S(2)}) copy-start(bf16[256,256]{1,0:T(8,128)(2,1)} %constant.15.clone.refs_7_) | copy-start | bytes 393220
  0.6 29.4 %copy-start.1 = (bf16[256,256]{1,0:T(8,128)(2,1)S(1)}, bf16[256,256]{1,0:T(8,128)(2,1)}, u32[]{:S(2)}) copy-start(bf16[256,256]{1,0:T(8,128)(2,1)} %constant.14.clone.refs_6_) | copy-start | bytes 393220
  0.7 29.4 %copy-start.2 = (bf16[1,3,2,256]{3,2,1,0:T(2,128)(2,1)S(1)}, bf16[1,3,2,256]{3,2,1,0:T(2,128)(2,1)}, u32[]{:S(2)}) copy-start(bf16[1,3,2,256]{3,2,1,0:T(2,128)(2,1)} %refs_1_.4) | copy-start | bytes 9220
  0.7 29.4 %copy-start.3 = (f32[8,128]{1,0:T(8,128)S(1)}, f32[8,128]{1,0:T(8,128)}, u32[]{:S(2)}) copy-start(f32[8,128]{1,0:T(8,128)} %constant.16.clone.refs_8_) | copy-start | bytes 12292
  0.7 29.4 %copy-start.4 = (s32[1,3,2]{1,2,0:T(2,128)S(1)}, s32[1,3,2]{1,2,0:T(2,128)}, u32[]{:S(2)}) copy-start(s32[1,3,2]{1,2,0:T(2,128)} %param.9) | copy-start | bytes 76
  0.7 29.4 %copy-start.6 = (s32[1,3]{1,0:T(1,128)S(1)}, s32[1,3]{1,0:T(1,128)}, u32[]{:S(2)}) copy-start(s32[1,3]{1,0:T(1,128)} %refs_3_.7) | copy-start | bytes 40
  4.2 22.0 %collective-permute-start = (bf16[49,32,256]{2,1,0:T(8,128)(2,1)}, bf16[49,32,256]{2,1,0:T(8,128)(2,1)S(1)}, u32[]{:S(2)}, u32[]{:S(2)}) collective-permute-start(bf16[49,32,256]{2,1,0:T(8,128)(2,1)} %get-tuple-element.39), channel_id=1, source_target_pairs={{0,4},{4,0},{8,12},{12,8},{16,20},{20,16},{24,28},{28,24},{1,5},{5... | collective-permute-start | bytes 2408456 | tf_op jit(solution)/shard_map/ppermute | solution.py:306
  7.2 22.9 %collective-permute-start.1 = (bf16[49,32,256]{2,1,0:T(8,128)(2,1)}, bf16[49,32,256]{2,1,0:T(8,128)(2,1)S(1)}, u32[]{:S(2)}, u32[]{:S(2)}) collective-permute-start(bf16[49,32,256]{2,1,0:T(8,128)(2,1)} %get-tuple-element.40), channel_id=1, source_target_pairs={{4,12},{8,0},{12,20},{16,8},{20,28},{24,16},{5,13},{9,1},{13,21},{... | collective-permute-start | bytes 2408456 | tf_op jit(solution)/shard_map/ppermute | solution.py:307
  11.6 27.2 %collective-permute-start.4 = (bf16[33,32,256]{2,1,0:T(8,128)(2,1)}, bf16[33,32,256]{2,1,0:T(8,128)(2,1)S(1)}, u32[]{:S(2)}, u32[]{:S(2)}) collective-permute-start(bf16[33,32,256]{2,1,0:T(8,128)(2,1)} %get-tuple-element.52), channel_id=1, source_target_pairs={{0,4},{4,0},{8,12},{12,8},{16,20},{20,16},{24,28},{28,24},{1,5},{5... | collective-permute-start | bytes 1622024 | tf_op jit(solution)/shard_map/ppermute | solution.py:306
  14.5 25.8 %collective-permute-start.5 = (bf16[33,32,256]{2,1,0:T(8,128)(2,1)}, bf16[33,32,256]{2,1,0:T(8,128)(2,1)S(1)}, u32[]{:S(2)}, u32[]{:S(2)}) collective-permute-start(bf16[33,32,256]{2,1,0:T(8,128)(2,1)} %get-tuple-element.53), channel_id=1, source_target_pairs={{4,12},{8,0},{12,20},{16,8},{20,28},{24,16},{5,13},{9,1},{13,21},{... | collective-permute-start | bytes 1622024 | tf_op jit(solution)/shard_map/ppermute | solution.py:307
  34.7 14.4 %collective-permute-start.2 = (f16[784,256]{1,0:T(8,128)(2,1)S(1)}, f16[784,256]{1,0:T(8,128)(2,1)S(1)}, u32[]{:S(2)}, u32[]{:S(2)}) collective-permute-start(f16[784,256]{1,0:T(8,128)(2,1)S(1)} %get-tuple-element.46), channel_id=1, source_target_pairs={{0,4},{4,0},{8,12},{12,8},{16,20},{20,16},{24,28},{28,24},{1,5},{5... | collective-permute-start | bytes 1204232 | tf_op jit(solution)/shard_map/ppermute | solution.py:338
  34.8 14.3 %collective-permute-start.3 = (f16[784,256]{1,0:T(8,128)(2,1)S(1)}, f16[784,256]{1,0:T(8,128)(2,1)S(1)}, u32[]{:S(2)}, u32[]{:S(2)}) collective-permute-start(f16[784,256]{1,0:T(8,128)(2,1)S(1)} %get-tuple-element.47), channel_id=1, source_target_pairs={{0,8},{8,16},{12,4},{16,24},{20,12},{28,20},{1,9},{9,17},{13,5},{1... | collective-permute-start | bytes 1204232 | tf_op jit(solution)/shard_map/ppermute | solution.py:339
  43.1 21.3 %copy-start.5 = (f32[2,256]{1,0:T(2,128)S(1)}, f32[2,256]{1,0:T(2,128)}, u32[]{:S(2)}) copy-start(f32[2,256]{1,0:T(2,128)} %qweight.3) | copy-start | bytes 6148
  45.0 8.6 %collective-permute-start.6 = (f16[528,256]{1,0:T(8,128)(2,1)S(1)}, f16[528,256]{1,0:T(8,128)(2,1)S(1)}, u32[]{:S(2)}, u32[]{:S(2)}) collective-permute-start(f16[528,256]{1,0:T(8,128)(2,1)S(1)} %multiply_convert_fusion.3), channel_id=1, source_target_pairs={{0,4},{4,0},{8,12},{12,8},{16,20},{20,16},{24,28},{28,24},{1,5},{5... | collective-permute-start | bytes 811016 | tf_op jit(solution)/shard_map/ppermute | solution.py:338
  45.1 8.5 %collective-permute-start.7 = (f16[528,256]{1,0:T(8,128)(2,1)S(1)}, f16[528,256]{1,0:T(8,128)(2,1)S(1)}, u32[]{:S(2)}, u32[]{:S(2)}) collective-permute-start(f16[528,256]{1,0:T(8,128)(2,1)S(1)} %multiply_convert_fusion.2), channel_id=1, source_target_pairs={{0,8},{8,16},{12,4},{16,24},{20,12},{28,20},{1,9},{9,17},{13,5},{1... | collective-permute-start | bytes 811016 | tf_op jit(solution)/shard_map/ppermute | solution.py:339
  50.1 10.8 %all-to-all-start = ((bf16[8,2,3,16,256]{4,3,2,1,0:T(8,128)(2,1)}), bf16[8,2,3,16,256]{4,3,2,1,0:T(8,128)(2,1)S(1)}, u32[]{:S(2)}, u32[]{:S(2)}) async-start(bf16[8,2,3,16,256]{4,3,2,1,0:T(8,128)(2,1)} %bitcast.7), calls=%async_computation | async-start | bytes 786432 | tf_op jit(solution)/shard_map/all_to_all | solution.py:351
  61.0 9.4 %all-to-all-start.1 = ((bf16[8,2,2,16,256]{4,3,2,1,0:T(8,128)(2,1)}), bf16[8,2,2,16,256]{4,3,2,1,0:T(8,128)(2,1)S(1)}, u32[]{:S(2)}, u32[]{:S(2)}) async-start(bf16[8,2,2,16,256]{4,3,2,1,0:T(8,128)(2,1)} %bitcast.11), calls=%async_computation.1 | async-start | bytes 524288 | tf_op jit(solution)/shard_map/all_to_all | solution.py:351
  71.5 13.3 %all-to-all-start.2 = ((f32[8,64,128]{2,1,0:T(8,128)}), f32[8,64,128]{2,1,0:T(8,128)S(1)}, u32[]{:S(2)}, u32[]{:S(2)}) async-start(f32[8,64,128]{2,1,0:T(8,128)} %gram.3), calls=%async_computation.2 | async-start | bytes 524288 | tf_op jit(solution)/shard_map/all_to_all | solution.py:382

commit v3 on v2

--- a/solution.py
+++ b/solution.py
@@ -66,37 +66,12 @@
     return rows
 
 
-def pack_body(chunk, plane_total, partials, weight, plane, count, near, far, hold, tail, sems):
-    first, width = chunk
+def weights_body(plane_total, weight, plane, count, own, near, far):
     parity = lax.rem(lax.axis_index("slab"), 2)
-    groups = hold.shape[1]
-    sides = (1, 2 * parity)
-    loads, stores = [], []
-    for place, side in enumerate(sides):
-        load = pltpu.make_async_copy(
-            partials.at[0, side, :, pl.ds(first, width)], hold.at[place], sems.at[place, groups]
-        )
-        load.start()
-        loads.append(load)
-    for place, (side, target) in enumerate(zip(sides, (near, far))):
+    for side, target in ((2 - 2 * parity, own), (1, near), (2 * parity, far)):
         rows = weight_rows(weight, plane, count, side, plane_total)
-        filler = jnp.zeros((tail.shape[1] - len(rows), tail.shape[2]), F32)
-        tail[place] = jnp.concatenate(rows + [filler], axis=0).astype(BF16)
-    for place, target in enumerate((near, far)):
-        loads[place].wait()
-        for g in range(groups):
-            store = pltpu.make_async_copy(
-                hold.at[place, g], target.at[pl.ds(g * width, width)], sems.at[place, g]
-            )
-            store.start()
-            stores.append(store)
-        store = pltpu.make_async_copy(
-            tail.at[place], target.at[groups * width], sems.at[place, groups + 1]
-        )
-        store.start()
-        stores.append(store)
-    for store in stores:
-        store.wait()
+        filler = jnp.zeros((target.shape[0] - len(rows), target.shape[1]), F32)
+        target[...] = jnp.concatenate(rows + [filler], axis=0).astype(BF16)
 
 
 def tap_sums(plane_total, start):
@@ -108,7 +83,7 @@
 
 
 def assemble_body(
-    dims, partials, weight, plane, count, near, far, dft, kyz, scales,
+    dims, partials, own_weight, near_weight, far_weight, near, far, dft, kyz, scales,
     kept_out, mid_out, outer_out, factor_out, own, near_hold, far_hold, grid, sems,
 ):
     first, width, plane_total, cap, blocks, times, points = dims
@@ -124,12 +99,9 @@
     ]
     for load in loads:
         load.start()
-    pieces = cap * blocks * width
-    own_rows = weight_rows(weight, plane, count, side, plane_total)
+    weights = [ref[...].astype(F32) for ref in (own_weight, near_weight, far_weight)]
     for load in loads:
         load.wait()
-    near_rows = near_hold[pieces].astype(F32)
-    far_rows = far_hold[pieces].astype(F32)
     rows = dft.shape[0] // 2
     height = 2 * blocks
     low = tap_sums(plane_total, 2 - plane_total)
@@ -141,16 +113,11 @@
             totals = [None] * plane_total
             for c in range(cap):
                 group = c * blocks + b
-                terms = (own[group, v], near_hold[group * width + v], far_hold[group * width + v])
-                for at, term in enumerate(terms):
-                    value = term.astype(F32)
+                for at, ref in enumerate((own, near_hold, far_hold)):
+                    value = ref[group, v].astype(F32)
                     for q in range(plane_total):
                         index = q * cap + c
-                        row = (
-                            own_rows[index],
-                            near_rows[index : index + 1],
-                            far_rows[index : index + 1],
-                        )[at]
+                        row = weights[at][index : index + 1]
                         product = value * row
                         totals[q] = product if totals[q] is None else totals[q] + product
             for q in range(plane_total):
@@ -176,23 +143,35 @@
                 part = jnp.maximum(jnp.abs(sent[i : i + 8]), jnp.abs(middle[i : i + 8]))
                 largest = jnp.maximum(largest, part)
             for k in range(rows // height):
-                start = ((k * plane_total + x) * width + v) * height
+                place = (k * plane_total + x) * width + v
                 for target, value in ((kept_out, kept), (mid_out, middle), (outer_out, sent)):
-                    target[start : start + height, :] = value[k * height : (k + 1) * height]
+                    target[place] = value[k * height : (k + 1) * height]
     largest = jnp.max(jnp.max(largest, axis=1, keepdims=True), axis=0, keepdims=True)
     passed = jnp.sum((largest >= scales[0:1, :]).astype(F32), axis=1, keepdims=True)
     lane = lax.broadcasted_iota(jnp.int32, (1, 128), 1).astype(F32)
     hit = lane == passed
     factor = jnp.sum(jnp.where(hit, scales[1:2, :], 0.0), axis=1, keepdims=True)
     mark = jnp.sum(jnp.where(hit, scales[2:3, :], 0.0), axis=1, keepdims=True)
-    total = plane_total * width * rows
     for target in (mid_out, outer_out):
-        target[total : total + 16, :] = jnp.broadcast_to(mark, (16, points))
+        target[target.shape[0] - 1] = jnp.broadcast_to(mark, (height, points))
     factor_out[...] = jnp.broadcast_to(factor, (8, 128))
 
 
-def gram_body(values, qweight, *refs):
-    *before, out = refs
+def partner(index, step, count):
+    return index ^ step if count & (count - 1) == 0 else lax.rem(index + step, count)
+
+
+def giver(index, step, count):
+    return partner(index, step if count & (count - 1) == 0 else count - step, count)
+
+
+def gram_body(pieces, *refs):
+    blocks, qweight, before, (values, out) = (
+        refs[:pieces], refs[pieces], refs[pieces + 1 : -2], refs[-2:],
+    )
+    me = lax.axis_index("freq")
+    for step, block in enumerate(blocks):
+        values[giver(me, step, pieces)] = block[...]
     sources, freqs, planes, variables, rows, points = values.shape
     columns = sources * rows
     results = []
@@ -275,7 +254,8 @@
     groups = cap * blocks
     natural = jnp.transpose(partials, (0, 1, 2, 3, 5, 4, 6))
     natural = natural.reshape(1, 3, groups, variables, times, points)
-    natural = pltpu.with_memory_space_constraint(natural, pltpu.HBM)
+    pinned = pltpu.with_memory_space_constraint(natural, pltpu.HBM)
+    parity = lax.rem(lax.axis_index("slab"), 2)
     planes = jnp.swapaxes(rec_plane, 1, 2)
     any_spec = pl.BlockSpec(memory_space=pl.ANY)
     hbm = pl.BlockSpec(memory_space=pltpu.HBM)
@@ -287,98 +267,118 @@
     columns = height * freqs
     chunks = chunks_of(variables)
 
-    def raw(chunk, weight):
+    def raw(chunk, token):
+        first, width = chunk
+        shape = (1, 1, groups, width, times, points)
+        near = lax.slice(natural, (0, 1, 0, first, 0, 0), (1, 2, groups, first + width, times, points))
+        near, token = lax.optimization_barrier((near, token))
+        far = lax.dynamic_slice(natural, (0, token, 0, first, 0, 0), shape)
+        far, token = lax.optimization_barrier((far, token))
+        return token, near.reshape(shape[2:]), far.reshape(shape[2:])
+
+    def assembled(chunk, weights, near, far):
         width = chunk[1]
-        payload = jax.ShapeDtypeStruct((groups * width + 1, times, points), BF16)
-        near, far = pl.pallas_call(
-            lambda *refs: pack_body(chunk, plane_total, *refs),
-            out_shape=(payload, payload),
-            in_specs=[hbm, vmem, smem, smem],
-            out_specs=(any_spec, any_spec),
-            scratch_shapes=[
-                pltpu.VMEM((2, groups, width, times, points), BF16),
-                pltpu.VMEM((2, times, points), BF16),
-                pltpu.SemaphoreType.DMA((2, groups + 2)),
-            ],
-            name="pack",
-        )(natural, weight, planes, rec_count)
-        weight, near, far = lax.optimization_barrier((weight, near, far))
-        near = lax.ppermute(near, "slab", pairs(slabs, 1, -1))
-        far = lax.ppermute(far, "slab", pairs(slabs, -2, 2))
-        return weight, (near, far)
-
-    def assembled(chunk, weight, near, far):
-        width = chunk[1]
-        total = NF * plane_total * width * height
+        total = NF * plane_total * width
         dims = chunk + (plane_total, cap, blocks, times, points)
+        held = pltpu.VMEM((groups, width, times, points), BF16)
+        message = jax.ShapeDtypeStruct((total + 1, height, points), F32)
         own, middle, outer, factor = pl.pallas_call(
             lambda *refs: assemble_body(dims, *refs),
             out_shape=(
-                jax.ShapeDtypeStruct((total, points), F32),
-                jax.ShapeDtypeStruct((total + 16, points), F32),
-                jax.ShapeDtypeStruct((total + 16, points), F32),
+                jax.ShapeDtypeStruct((total, height, points), F32),
+                message,
+                message,
                 jax.ShapeDtypeStruct((8, 128), F32),
             ),
-            in_specs=[hbm, vmem, smem, smem, any_spec, any_spec] + [vmem] * 3,
+            in_specs=[hbm] + [vmem] * 3 + [any_spec] * 2 + [vmem] * 3,
             out_specs=(vmem,) * 4,
             scratch_shapes=[
-                pltpu.VMEM((groups, width, times, points), BF16),
-                pltpu.VMEM((groups * width + 1, times, points), BF16),
-                pltpu.VMEM((groups * width + 1, times, points), BF16),
+                held,
+                held,
+                held,
                 pltpu.VMEM((plane_total, blocks * times, points), BF16),
                 pltpu.SemaphoreType.DMA((3,)),
             ],
             compiler_params=PARAMS,
             name="assemble",
-        )(natural, weight, planes, rec_count, near, far, dft, kyz, scales)
+        )(pinned, *weights, near, far, dft, kyz, scales)
         middle, outer = (
             (value * factor[0, 0]).astype(jnp.float16) for value in (middle, outer)
         )
-        weight, own, middle, outer = lax.optimization_barrier((weight, own, middle, outer))
-        middle = lax.ppermute(middle, "slab", pairs(slabs, 1, -1))
+        weights, own, middle, outer = lax.optimization_barrier((weights, own, middle, outer))
+        middle = lax.ppermute(middle, "slab", swap)
         outer = lax.ppermute(outer, "slab", pairs(slabs, 2, -2))
-        return weight, (own, middle, outer)
+        return weights, (own, middle, outer)
 
     def combined(chunk, token, own, middle, outer):
         width = chunk[1]
-        total = own.shape[0]
         own, middle, outer, token = lax.optimization_barrier((own, middle, outer, token))
-        for message in (middle, outer):
-            scale = jnp.exp2(message[total : total + 1].astype(F32) - F16_LOG2)
-            own = own + message[:total].astype(F32) * scale
-        own = own.astype(BF16)
-        local = own.reshape(NF, plane_total, width, height, points)
-        values = lax.all_to_all(local, "freq", split_axis=0, concat_axis=0, tiled=True)
-        return own, values.reshape(freqs, kept, plane_total, width, height, points)
-
-    def partial_gram(values, before, copies):
+        scales = [jnp.exp2(m[-1:, :1].astype(F32) - F16_LOG2) for m in (middle, outer)]
+        size = kept * plane_total * width
+        parts = []
+        for step in range(freqs):
+            start = partner(lax.axis_index("freq"), step, freqs) * size
+            value = lax.dynamic_slice_in_dim(own, start, size, 0)
+            for message, scale in zip((middle, outer), scales):
+                value = value + lax.dynamic_slice_in_dim(message, start, size, 0) * scale
+            parts.append(value.astype(BF16))
+        parts = lax.optimization_barrier(tuple(parts))
+        token = parts[0]
+        arrived = []
+        for step, value in enumerate(parts):
+            if step:
+                route = [(f, int(partner(np.int64(f), step, freqs))) for f in range(freqs)]
+                value = lax.ppermute(value, "freq", route)
+            arrived.append(value.reshape(kept, plane_total, width, height, points))
+        return token, arrived
+
+    def partial_gram(blocks, before, copies):
         return pl.pallas_call(
-            gram_body,
-            out_shape=jax.ShapeDtypeStruct((copies, columns, kept * columns), F32),
-            in_specs=[vmem] * (2 + len(before)),
-            out_specs=vmem,
+            lambda *refs: gram_body(freqs, *refs),
+            out_shape=(
+                jax.ShapeDtypeStruct((freqs,) + blocks[0].shape, BF16),
+                jax.ShapeDtypeStruct((copies, columns, kept * columns), F32),
+            ),
+            in_specs=[vmem] * (freqs + 1 + len(before)),
+            out_specs=(vmem, vmem),
             compiler_params=PARAMS,
             name="gram",
-        )(values, qweight, *before)
-
+        )(*blocks, qweight, *before)
+
+    swap = pairs(slabs, 1, -1)
+    onward = pairs(slabs, -2, 2)
     arrived = []
-    weight = rec_weight
+    token = 2 * parity
     for chunk in chunks:
-        weight, records = raw(chunk, weight)
-        arrived.append(records)
+        token, near, far = raw(chunk, token)
+        arrived.append((lax.ppermute(near, "slab", swap), lax.ppermute(far, "slab", onward)))
+    small = jax.ShapeDtypeStruct((16, points), BF16)
+    weights = pl.pallas_call(
+        lambda *refs: weights_body(plane_total, *refs),
+        out_shape=(small,) * 3,
+        in_specs=[vmem, smem, smem],
+        out_specs=(vmem,) * 3,
+        name="weights",
+    )(rec_weight, planes, rec_count)
+    weights = (
+        weights[0],
+        lax.ppermute(weights[1], "slab", swap),
+        lax.ppermute(weights[2], "slab", onward),
+    )
     sent = []
     for chunk, records in zip(chunks, arrived):
-        weight, parts = assembled(chunk, weight, *records)
+        weights, parts = assembled(chunk, weights, *records)
         sent.append(parts)
     values = []
     token = qweight
     for chunk, parts in zip(chunks, sent):
-        token, value = combined(chunk, token, *parts)
-        values.append(value)
+        token, blocks_of = combined(chunk, token, *parts)
+        values.append(blocks_of)
     gram = ()
     for at, value in enumerate(values):
         copies = slabs if at == len(values) - 1 else 1
-        gram = (partial_gram(value, gram, copies),)
+        values[at], result = partial_gram(value, gram, copies)
+        gram = (result,)
     grams = lax.all_to_all(gram[0], "slab", split_axis=0, concat_axis=0, tiled=True)
     factor = pl.pallas_call(
         lambda *refs: factor_body(kept, *refs),

time: 87.9 us -> 92.6 us (1.053)
  local copies, waits for them, and re-layouts: 1.91 us -> 10.6 us
  Pallas kernels: 16.8 us -> 10.6 us
  waiting for transfers between devices: 33.7 us -> 38.1 us
  other arithmetic: 5.74 us -> 2.78 us
    ppermute x6 -> x14, waiting for transfers between devices: 15.7 us -> 29.6 us  [the longest x1 20.9 us: body(): lax.ppermute(weights[1], 'slab', swap)]
    all_to_all x2 -> x0, waiting for transfers between devices: 11.9 us -> none  [combined(): lax.all_to_all(local, 'freq', split_axis=0, concat_axis=0, tiled=True)]
    ppermute x6 -> x14, starting transfers between devices: 8.57 us -> 16.3 us  [the longest x2 7.53 us: body(): lax.ppermute(near, 'slab', swap)]
    all_to_all x2 -> x0, starting transfers between devices: 6.86 us -> none  [combined(): lax.all_to_all(local, 'freq', split_axis=0, concat_axis=0, tiled=True)]
    pallas_call x4 -> x3, Pallas kernels: 8.26 us -> 3.18 us  [the longest x2 1.72 us: partial_gram(): pl.pallas_call(lambda *refs: gram_body(freqs, *refs), out_shape=(jax.Shap...]
    dynamic_slice x0 -> x2, local copies, waits for them, and re-layouts: none -> 4.02 us  [raw(): far = lax.dynamic_slice(natural, (0, token, 0, first, 0, 0), shape)]
    slice x0 -> x2, local copies, waits for them, and re-layouts: none -> 3.25 us  [raw(): lax.slice(natural, (0, 1, 0, first, 0, 0), (1, 2, groups, first + width,...]
    concatenate x1, other arithmetic: 1.68 us -> 0.06 us  [body(): spectra = jnp.concatenate(values, axis=3)]
  transfers between devices with their start and end apart: 11 -> 17, of which waited for: 6 -> 9; matrix products, arithmetic and copies ran while one was open for 9% -> 9% of each run, Pallas kernels for 11% -> 8%
where the time goes in v3:
time: 92.6 us; the launch traced here: 92 us
  waiting for transfers between devices  38.1 us (41%)
  starting transfers between devices  28.9 us (31%)
  local copies, waits for them, and re-layouts  10.6 us (11%)
  Pallas kernels  10.6 us (11%)
  other arithmetic  2.78 us (3%)
  between operations  0.95 us (1%)
    ppermute x1, waiting for transfers between devices, body(): lax.ppermute(weights[1], 'slab', swap)  20.9 us
    ppermute x2, starting transfers between devices, assembled(): outer = lax.ppermute(outer, 'slab', pairs(slabs, 2, -2))  7.68 us
    all_to_all x1, waiting for transfers between devices, body(): lax.all_to_all(gram[0], 'slab', split_axis=0, concat_axis=0, tiled=True)  7.56 us
    ppermute x2, starting transfers between devices, body(): lax.ppermute(near, 'slab', swap)  7.53 us
    pallas_call x2, Pallas kernels, assembled(): pl.pallas_call(lambda *refs: assemble_body(dims, *refs), out_shape=(jax.S...  4.98 us
    all_to_all x1, starting transfers between devices, body(): lax.all_to_all(gram[0], 'slab', split_axis=0, concat_axis=0, tiled=True)  4.86 us
    ppermute x1, waiting for transfers between devices, body(): lax.ppermute(weights[2], 'slab', onward)  4.4 us
    dynamic_slice x2, local copies, waits for them, and re-layouts, raw(): far = lax.dynamic_slice(natural, (0, token, 0, first, 0, 0), shape)  4.02 us
  transfers between devices with their start and end apart: 17, of which 9 were waited for; matrix products, arithmetic and copies ran while one was open for 9% of the time, Pallas kernels for 8%

profile of v3, /device:TPU:0, one launch (start us, length us, event | category | flops | bytes accessed | tf_op | source)
XLA Modules:
  0.0 92.0 jit_solution(242855033150148186)
XLA Ops:
  0.7 2.2 %slice.34 = bf16[1,1,16,3,32,256]{5,4,3,2,1,0:T(8,128)(2,1)} slice(bf16[1,3,16,5,32,256]{5,4,3,2,1,0:T(8,128)(2,1)} %bitcast.34), slice={[0:1], [1:2], [0:16], [0:3], [0:32], [0:256]} | slice | bytes 1572864 | tf_op jit(solution)/shard_map/slice | solution.py:273
  2.8 2.1 %constant_dynamic-slice_fusion.1 = bf16[1,1,16,3,32,256]{5,4,3,2,1,0:T(8,128)(2,1)} fusion(bf16[1,3,16,5,32,256]{5,4,3,2,1,0:T(8,128)(2,1)} %bitcast.35, s32[]{:T(128)S(6)} %select_n.62), kind=kLoop, calls=%fused_computation.14 | loop fusion | bytes 1572868 | tf_op jit(solution)/shard_map/dynamic_slice | solution.py:275
  5.0 1.3 %collective-permute-start.3 = (bf16[16,3,32,256]{3,2,1,0:T(8,128)(2,1)}, bf16[16,3,32,256]{3,2,1,0:T(8,128)(2,1)S(1)}, u32[]{:S(2)}, u32[]{:S(2)}) collective-permute-start(bf16[16,3,32,256]{3,2,1,0:T(8,128)(2,1)} %bitcast.5), channel_id=1, source_target_pairs={{4,12},{8,0},{12,20},{16,8},{20,28},{24,16},{5,13},{9,1},{13,21},{... | collective-permute-start | bytes 2359304 | tf_op jit(solution)/shard_map/ppermute | solution.py:354
  6.3 5.3 %collective-permute-start.2 = (bf16[16,3,32,256]{3,2,1,0:T(8,128)(2,1)}, bf16[16,3,32,256]{3,2,1,0:T(8,128)(2,1)S(1)}, u32[]{:S(2)}, u32[]{:S(2)}) collective-permute-start(bf16[16,3,32,256]{3,2,1,0:T(8,128)(2,1)} %bitcast.4), channel_id=1, source_target_pairs={{0,4},{4,0},{8,12},{12,8},{16,20},{20,16},{24,28},{28,24},{1,5},{5... | collective-permute-start | bytes 2359304 | tf_op jit(solution)/shard_map/ppermute | solution.py:354
  11.5 1.1 %slice.35 = bf16[1,1,16,2,32,256]{5,4,3,2,1,0:T(8,128)(2,1)S(1)} slice(bf16[1,3,16,5,32,256]{5,4,3,2,1,0:T(8,128)(2,1)} %bitcast.36), slice={[0:1], [1:2], [0:16], [3:5], [0:32], [0:256]} | slice | bytes 1048576 | tf_op jit(solution)/shard_map/slice | solution.py:273
  12.6 1.9 %constant_dynamic-slice_fusion = bf16[1,1,16,2,32,256]{5,4,3,2,1,0:T(8,128)(2,1)} fusion(bf16[1,3,16,5,32,256]{5,4,3,2,1,0:T(8,128)(2,1)} %bitcast.37, s32[]{:T(128)S(6)} %select_n.71), kind=kLoop, calls=%fused_computation.13 | loop fusion | bytes 1048580 | tf_op jit(solution)/shard_map/dynamic_slice | solution.py:275
  14.5 1.3 %collective-permute-start.10 = (bf16[16,2,32,256]{3,2,1,0:T(8,128)(2,1)}, bf16[16,2,32,256]{3,2,1,0:T(8,128)(2,1)S(1)}, u32[]{:S(2)}, u32[]{:S(2)}) collective-permute-start(bf16[16,2,32,256]{3,2,1,0:T(8,128)(2,1)} %bitcast.14), channel_id=1, source_target_pairs={{4,12},{8,0},{12,20},{16,8},{20,28},{24,16},{5,13},{9,1},{13,21},{... | collective-permute-start | bytes 1572872 | tf_op jit(solution)/shard_map/ppermute | solution.py:354
  15.8 2.3 %collective-permute-start.9 = (bf16[16,2,32,256]{3,2,1,0:T(8,128)(2,1)S(1)}, bf16[16,2,32,256]{3,2,1,0:T(8,128)(2,1)S(1)}, u32[]{:S(2)}, u32[]{:S(2)}) collective-permute-start(bf16[16,2,32,256]{3,2,1,0:T(8,128)(2,1)S(1)} %bitcast.42), channel_id=1, source_target_pairs={{0,4},{4,0},{8,12},{12,8},{16,20},{20,16},{24,28},{28,24},{1,5},{5... | collective-permute-start | bytes 1572872 | tf_op jit(solution)/shard_map/ppermute | solution.py:354
  18.1 1.5 %weights.1 = (bf16[16,256]{1,0:T(8,128)(2,1)}, bf16[16,256]{1,0:T(8,128)(2,1)}, bf16[16,256]{1,0:T(8,128)(2,1)}) custom-call(bf16[1,3,2,256]{3,2,1,0:T(2,128)(2,1)} %refs_0_.1, s32[1,2,3]{2,1,0:T(2,128)} %bitcast.47, s32[1,3]{1,0:T(1,128)} %refs_2_.1), custom_call_target="tpu_custom_call" | custom-call | tf_op jit(solution)/shard_map/weights/pallas_call | solution.py:356
  19.5 20.9 %collective-permute-done.refs_2_ = bf16[16,256]{1,0:T(8,128)(2,1)S(1)} collective-permute-done((bf16[16,256]{1,0:T(8,128)(2,1)}, bf16[16,256]{1,0:T(8,128)(2,1)S(1)}, u32[]{:S(2)}, u32[]{:S(2)}) %collective-permute-start) | collective-permute-done | bytes 8224 | tf_op jit(solution)/shard_map/ppermute | solution.py:365
  40.4 1.3 %collective-permute-start.1 = (bf16[16,256]{1,0:T(8,128)(2,1)}, bf16[16,256]{1,0:T(8,128)(2,1)S(1)}, u32[]{:S(2)}, u32[]{:S(2)}) collective-permute-start(bf16[16,256]{1,0:T(8,128)(2,1)} %get-tuple-element.49), channel_id=1, source_target_pairs={{4,12},{8,0},{12,20},{16,8},{20,28},{24,16},{5,13},{9,1},{13,21},{... | collective-permute-start | bytes 24584 | tf_op jit(solution)/shard_map/ppermute | solution.py:366
  41.8 4.4 %collective-permute-done.1.refs_3_ = bf16[16,256]{1,0:T(8,128)(2,1)S(1)} collective-permute-done((bf16[16,256]{1,0:T(8,128)(2,1)}, bf16[16,256]{1,0:T(8,128)(2,1)S(1)}, u32[]{:S(2)}, u32[]{:S(2)}) %collective-permute-start.1) | collective-permute-done | bytes 8224 | tf_op jit(solution)/shard_map/ppermute | solution.py:366
  46.9 2.7 %assemble.2 = (f32[48,16,256]{2,1,0:T(8,128)S(1)}, f32[49,16,256]{2,1,0:T(8,128)S(1)}, f32[49,16,256]{2,1,0:T(8,128)S(1)}, f32[8,128]{1,0:T(8,128)S(1)}) custom-call(bf16[1,3,16,5,32,256]{5,4,3,2,1,0:T(8,128)(2,1)} %bitcast.38, bf16[16,256]{1,0:T(8,128)(2,1)S(1)} %copy-done.2, bf16[16,256]{1,0:T(8,128)(2,1)S(1)} %collective-permute-done.refs_2_, ...), custom_call_target="tpu_custom_call" | custom-call | tf_op jit(solution)/shard_map/assemble/pallas_call | solution.py:285
  50.1 0.9 multiply_convert_fusion
  51.0 1.1 %collective-permute-start.4 = (f16[49,16,256]{2,1,0:T(8,128)(2,1)S(1)}, f16[49,16,256]{2,1,0:T(8,128)(2,1)S(1)}, u32[]{:S(2)}, u32[]{:S(2)}) collective-permute-start(f16[49,16,256]{2,1,0:T(8,128)(2,1)S(1)} %get-tuple-element.58), channel_id=1, source_target_pairs={{0,4},{4,0},{8,12},{12,8},{16,20},{20,16},{24,28},{28,24},{1,5},{5... | collective-permute-start | bytes 1204232 | tf_op jit(solution)/shard_map/ppermute | solution.py:309
  52.1 4.2 %collective-permute-start.5 = (f16[49,16,256]{2,1,0:T(8,128)(2,1)S(1)}, f16[49,16,256]{2,1,0:T(8,128)(2,1)S(1)}, u32[]{:S(2)}, u32[]{:S(2)}) collective-permute-start(f16[49,16,256]{2,1,0:T(8,128)(2,1)S(1)} %get-tuple-element.59), channel_id=1, source_target_pairs={{0,8},{8,16},{12,4},{16,24},{20,12},{28,20},{1,9},{9,17},{13,5},{1... | collective-permute-start | bytes 1204232 | tf_op jit(solution)/shard_map/ppermute | solution.py:310
  56.3 2.3 %assemble.3 = (f32[32,16,256]{2,1,0:T(8,128)S(1)}, f32[33,16,256]{2,1,0:T(8,128)S(1)}, f32[33,16,256]{2,1,0:T(8,128)S(1)}, f32[8,128]{1,0:T(8,128)S(1)}) custom-call(bf16[1,3,16,5,32,256]{5,4,3,2,1,0:T(8,128)(2,1)} %bitcast.39, bf16[16,256]{1,0:T(8,128)(2,1)S(1)} %copy-done.2, bf16[16,256]{1,0:T(8,128)(2,1)S(1)} %collective-permute-done.refs_2_, ...), custom_call_target="tpu_custom_call" | custom-call | tf_op jit(solution)/shard_map/assemble/pallas_call | solution.py:285
  59.1 0.7 multiply_convert_fusion.2
  59.8 0.7 multiply_convert_fusion.3
  60.6 3.5 %collective-permute-start.12 = (f16[33,16,256]{2,1,0:T(8,128)(2,1)S(1)}, f16[33,16,256]{2,1,0:T(8,128)(2,1)S(1)}, u32[]{:S(2)}, u32[]{:S(2)}) collective-permute-start(f16[33,16,256]{2,1,0:T(8,128)(2,1)S(1)} %multiply_convert_fusion.2), channel_id=1, source_target_pairs={{0,8},{8,16},{12,4},{16,24},{20,12},{28,20},{1,9},{9,17},{13,5},{1... | collective-permute-start | bytes 811016 | tf_op jit(solution)/shard_map/ppermute | solution.py:310
  64.4 1.6 %collective-permute-start.7 = (bf16[12,16,256]{2,1,0:T(8,128)(2,1)S(1)}, bf16[12,16,256]{2,1,0:T(8,128)(2,1)S(1)}, u32[]{:S(2)}, u32[]{:S(2)}) collective-permute-start(bf16[12,16,256]{2,1,0:T(8,128)(2,1)S(1)} %get-tuple-element.65), channel_id=1, source_target_pairs={{0,2},{1,3},{2,0},{3,1},{4,6},{5,7},{6,4},{7,5},{8,10},{9,11},{10,... | collective-permute-start | bytes 294920 | tf_op jit(solution)/shard_map/ppermute | solution.py:331
  66.3 0.7 collective-permute-done.11
  67.0 1.0 %collective-permute-done.12 = f16[33,16,256]{2,1,0:T(8,128)(2,1)S(1)} collective-permute-done((f16[33,16,256]{2,1,0:T(8,128)(2,1)S(1)}, f16[33,16,256]{2,1,0:T(8,128)(2,1)S(1)}, u32[]{:S(2)}, u32[]{:S(2)}) %collective-permute-start.12) | collective-permute-done | bytes 270368 | tf_op jit(solution)/shard_map/ppermute | solution.py:310
  68.3 1.6 %collective-permute-start.14 = (bf16[8,16,256]{2,1,0:T(8,128)(2,1)S(1)}, bf16[8,16,256]{2,1,0:T(8,128)(2,1)S(1)}, u32[]{:S(2)}, u32[]{:S(2)}) collective-permute-start(bf16[8,16,256]{2,1,0:T(8,128)(2,1)S(1)} %get-tuple-element.87), channel_id=1, source_target_pairs={{0,2},{1,3},{2,0},{3,1},{4,6},{5,7},{6,4},{7,5},{8,10},{9,11},{10,... | collective-permute-start | bytes 196616 | tf_op jit(solution)/shard_map/ppermute | solution.py:331
  70.2 1.0 %collective-permute-done.8 = bf16[12,16,256]{2,1,0:T(8,128)(2,1)S(1)} collective-permute-done((bf16[12,16,256]{2,1,0:T(8,128)(2,1)S(1)}, bf16[12,16,256]{2,1,0:T(8,128)(2,1)S(1)}, u32[]{:S(2)}, u32[]{:S(2)}) %collective-permute-start.8) | collective-permute-done | bytes 98336 | tf_op jit(solution)/shard_map/ppermute | solution.py:331
  71.8 1.7 %collective-permute-done.14 = bf16[8,16,256]{2,1,0:T(8,128)(2,1)S(1)} collective-permute-done((bf16[8,16,256]{2,1,0:T(8,128)(2,1)S(1)}, bf16[8,16,256]{2,1,0:T(8,128)(2,1)S(1)}, u32[]{:S(2)}, u32[]{:S(2)}) %collective-permute-start.14) | collective-permute-done | bytes 65568 | tf_op jit(solution)/shard_map/ppermute | solution.py:331
  73.4 0.8 collective-permute-done.15
  74.2 1.2 %gram.3 = (bf16[4,2,2,2,16,256]{5,4,3,2,1,0:T(8,128)(2,1)S(1)}, f32[8,64,128]{2,1,0:T(8,128)}) custom-call(bf16[2,2,2,16,256]{4,3,2,1,0:T(8,128)(2,1)S(1)} %bitcast.27, bf16[2,2,2,16,256]{4,3,2,1,0:T(8,128)(2,1)S(1)} %bitcast.31, bf16[2,2,2,16,256]{4,3,2,1,0:T(8,128)(2,1)S(1)} %bitcast.32, bf16[2,2,2,16,256]{4,3,2,1,0:T(8,128)(2,1)S(1)} %bitcast.33, ...), custom_call_target="tpu_custom_call" | custom-call | tf_op jit(solution)/shard_map/gram/pallas_call | solution.py:336
  75.4 4.9 %all-to-all-start = ((f32[8,64,128]{2,1,0:T(8,128)}), f32[8,64,128]{2,1,0:T(8,128)S(1)}, u32[]{:S(2)}, u32[]{:S(2)}) async-start(f32[8,64,128]{2,1,0:T(8,128)} %get-tuple-element.91), calls=%async_computation | async-start | bytes 524288 | tf_op jit(solution)/shard_map/all_to_all | solution.py:382
  80.6 1.4 %copy.10 = bf16[2,4,8,2,2,5,256]{6,4,5,3,2,1,0:T(2,128)(2,1)} copy(bf16[2,4,8,2,2,5,256]{6,3,2,5,4,0,1:T(2,128)(2,1)S(1)} %bitcast.40) | data formatting | bytes 1310720 | tf_op jit(solution)/shard_map/transpose | solution.py:393
  81.9 7.6 %all-to-all-done.refs_0_ = f32[8,64,128]{2,1,0:T(8,128)S(1)} async-done(((f32[8,64,128]{2,1,0:T(8,128)}), f32[8,64,128]{2,1,0:T(8,128)S(1)}, u32[]{:S(2)}, u32[]{:S(2)}) %all-to-all-start) | async-done | bytes 262176 | tf_op jit(solution)/shard_map/all_to_all | solution.py:382
  89.5 2.5 %factor.1 = f32[2,64,64]{2,1,0:T(8,128)} custom-call(f32[8,64,128]{2,1,0:T(8,128)S(1)} %all-to-all-done.refs_0_), custom_call_target="tpu_custom_call" | custom-call | tf_op jit(solution)/shard_map/factor/pallas_call | solution.py:383
  (36 shorter events, 3.9 us)
Async XLA Ops:
  0.6 45.5 %copy-start = (bf16[256,256]{1,0:T(8,128)(2,1)S(1)}, bf16[256,256]{1,0:T(8,128)(2,1)}, u32[]{:S(2)}) copy-start(bf16[256,256]{1,0:T(8,128)(2,1)} %constant.45.clone.refs_6_) | copy-start | bytes 393220
  0.6 45.5 %copy-start.1 = (bf16[256,256]{1,0:T(8,128)(2,1)S(1)}, bf16[256,256]{1,0:T(8,128)(2,1)}, u32[]{:S(2)}) copy-start(bf16[256,256]{1,0:T(8,128)(2,1)} %constant.46.clone.refs_7_) | copy-start | bytes 393220
  0.7 45.5 %copy-start.3 = (f32[8,128]{1,0:T(8,128)S(1)}, f32[8,128]{1,0:T(8,128)}, u32[]{:S(2)}) copy-start(f32[8,128]{1,0:T(8,128)} %constant.47.clone.refs_8_) | copy-start | bytes 12292
  5.0 41.2 %collective-permute-start.3 = (bf16[16,3,32,256]{3,2,1,0:T(8,128)(2,1)}, bf16[16,3,32,256]{3,2,1,0:T(8,128)(2,1)S(1)}, u32[]{:S(2)}, u32[]{:S(2)}) collective-permute-start(bf16[16,3,32,256]{3,2,1,0:T(8,128)(2,1)} %bitcast.5), channel_id=1, source_target_pairs={{4,12},{8,0},{12,20},{16,8},{20,28},{24,16},{5,13},{9,1},{13,21},{... | collective-permute-start | bytes 2359304 | tf_op jit(solution)/shard_map/ppermute | solution.py:354
  6.3 39.9 %collective-permute-start.2 = (bf16[16,3,32,256]{3,2,1,0:T(8,128)(2,1)}, bf16[16,3,32,256]{3,2,1,0:T(8,128)(2,1)S(1)}, u32[]{:S(2)}, u32[]{:S(2)}) collective-permute-start(bf16[16,3,32,256]{3,2,1,0:T(8,128)(2,1)} %bitcast.4), channel_id=1, source_target_pairs={{0,4},{4,0},{8,12},{12,8},{16,20},{20,16},{24,28},{28,24},{1,5},{5... | collective-permute-start | bytes 2359304 | tf_op jit(solution)/shard_map/ppermute | solution.py:354
  14.5 41.7 %collective-permute-start.10 = (bf16[16,2,32,256]{3,2,1,0:T(8,128)(2,1)}, bf16[16,2,32,256]{3,2,1,0:T(8,128)(2,1)S(1)}, u32[]{:S(2)}, u32[]{:S(2)}) collective-permute-start(bf16[16,2,32,256]{3,2,1,0:T(8,128)(2,1)} %bitcast.14), channel_id=1, source_target_pairs={{4,12},{8,0},{12,20},{16,8},{20,28},{24,16},{5,13},{9,1},{13,21},{... | collective-permute-start | bytes 1572872 | tf_op jit(solution)/shard_map/ppermute | solution.py:354
  15.8 40.5 %collective-permute-start.9 = (bf16[16,2,32,256]{3,2,1,0:T(8,128)(2,1)S(1)}, bf16[16,2,32,256]{3,2,1,0:T(8,128)(2,1)S(1)}, u32[]{:S(2)}, u32[]{:S(2)}) collective-permute-start(bf16[16,2,32,256]{3,2,1,0:T(8,128)(2,1)S(1)} %bitcast.42), channel_id=1, source_target_pairs={{0,4},{4,0},{8,12},{12,8},{16,20},{20,16},{24,28},{28,24},{1,5},{5... | collective-permute-start | bytes 1572872 | tf_op jit(solution)/shard_map/ppermute | solution.py:354
  19.5 20.9 %collective-permute-start = (bf16[16,256]{1,0:T(8,128)(2,1)}, bf16[16,256]{1,0:T(8,128)(2,1)S(1)}, u32[]{:S(2)}, u32[]{:S(2)}) collective-permute-start(bf16[16,256]{1,0:T(8,128)(2,1)} %get-tuple-element.48), channel_id=1, source_target_pairs={{0,4},{4,0},{8,12},{12,8},{16,20},{20,16},{24,28},{28,24},{1,5},{5... | collective-permute-start | bytes 24584 | tf_op jit(solution)/shard_map/ppermute | solution.py:365
  40.4 5.7 %collective-permute-start.1 = (bf16[16,256]{1,0:T(8,128)(2,1)}, bf16[16,256]{1,0:T(8,128)(2,1)S(1)}, u32[]{:S(2)}, u32[]{:S(2)}) collective-permute-start(bf16[16,256]{1,0:T(8,128)(2,1)} %get-tuple-element.49), channel_id=1, source_target_pairs={{4,12},{8,0},{12,20},{16,8},{20,28},{24,16},{5,13},{9,1},{13,21},{... | collective-permute-start | bytes 24584 | tf_op jit(solution)/shard_map/ppermute | solution.py:366
  46.2 0.7 copy-start.2
  51.0 20.2 %copy-start.4 = (f32[2,256]{1,0:T(2,128)S(1)}, f32[2,256]{1,0:T(2,128)}, u32[]{:S(2)}) copy-start(f32[2,256]{1,0:T(2,128)} %refs_4_.3) | copy-start | bytes 6148
  51.0 13.1 %collective-permute-start.4 = (f16[49,16,256]{2,1,0:T(8,128)(2,1)S(1)}, f16[49,16,256]{2,1,0:T(8,128)(2,1)S(1)}, u32[]{:S(2)}, u32[]{:S(2)}) collective-permute-start(f16[49,16,256]{2,1,0:T(8,128)(2,1)S(1)} %get-tuple-element.58), channel_id=1, source_target_pairs={{0,4},{4,0},{8,12},{12,8},{16,20},{20,16},{24,28},{28,24},{1,5},{5... | collective-permute-start | bytes 1204232 | tf_op jit(solution)/shard_map/ppermute | solution.py:309
  52.1 12.0 %collective-permute-start.5 = (f16[49,16,256]{2,1,0:T(8,128)(2,1)S(1)}, f16[49,16,256]{2,1,0:T(8,128)(2,1)S(1)}, u32[]{:S(2)}, u32[]{:S(2)}) collective-permute-start(f16[49,16,256]{2,1,0:T(8,128)(2,1)S(1)} %get-tuple-element.59), channel_id=1, source_target_pairs={{0,8},{8,16},{12,4},{16,24},{20,12},{28,20},{1,9},{9,17},{13,5},{1... | collective-permute-start | bytes 1204232 | tf_op jit(solution)/shard_map/ppermute | solution.py:310
  60.5 6.5 %collective-permute-start.11 = (f16[33,16,256]{2,1,0:T(8,128)(2,1)S(1)}, f16[33,16,256]{2,1,0:T(8,128)(2,1)S(1)}, u32[]{:S(2)}, u32[]{:S(2)}) collective-permute-start(f16[33,16,256]{2,1,0:T(8,128)(2,1)S(1)} %multiply_convert_fusion.3), channel_id=1, source_target_pairs={{0,4},{4,0},{8,12},{12,8},{16,20},{20,16},{24,28},{28,24},{1,5},{5... | collective-permute-start | bytes 811016 | tf_op jit(solution)/shard_map/ppermute | solution.py:309
  60.6 7.4 %collective-permute-start.12 = (f16[33,16,256]{2,1,0:T(8,128)(2,1)S(1)}, f16[33,16,256]{2,1,0:T(8,128)(2,1)S(1)}, u32[]{:S(2)}, u32[]{:S(2)}) collective-permute-start(f16[33,16,256]{2,1,0:T(8,128)(2,1)S(1)} %multiply_convert_fusion.2), channel_id=1, source_target_pairs={{0,8},{8,16},{12,4},{16,24},{20,12},{28,20},{1,9},{9,17},{13,5},{1... | collective-permute-start | bytes 811016 | tf_op jit(solution)/shard_map/ppermute | solution.py:310
  64.4 5.5 %collective-permute-start.6 = (bf16[12,16,256]{2,1,0:T(8,128)(2,1)S(1)}, bf16[12,16,256]{2,1,0:T(8,128)(2,1)S(1)}, u32[]{:S(2)}, u32[]{:S(2)}) collective-permute-start(bf16[12,16,256]{2,1,0:T(8,128)(2,1)S(1)} %get-tuple-element.64), channel_id=1, source_target_pairs={{0,1},{1,0},{2,3},{3,2},{4,5},{5,4},{6,7},{7,6},{8,9},{9,8},{10,11... | collective-permute-start | bytes 294920 | tf_op jit(solution)/shard_map/ppermute | solution.py:331
  64.4 5.7 %collective-permute-start.7 = (bf16[12,16,256]{2,1,0:T(8,128)(2,1)S(1)}, bf16[12,16,256]{2,1,0:T(8,128)(2,1)S(1)}, u32[]{:S(2)}, u32[]{:S(2)}) collective-permute-start(bf16[12,16,256]{2,1,0:T(8,128)(2,1)S(1)} %get-tuple-element.65), channel_id=1, source_target_pairs={{0,2},{1,3},{2,0},{3,1},{4,6},{5,7},{6,4},{7,5},{8,10},{9,11},{10,... | collective-permute-start | bytes 294920 | tf_op jit(solution)/shard_map/ppermute | solution.py:331
  66.0 5.2 %collective-permute-start.8 = (bf16[12,16,256]{2,1,0:T(8,128)(2,1)S(1)}, bf16[12,16,256]{2,1,0:T(8,128)(2,1)S(1)}, u32[]{:S(2)}, u32[]{:S(2)}) collective-permute-start(bf16[12,16,256]{2,1,0:T(8,128)(2,1)S(1)} %get-tuple-element.66), channel_id=1, source_target_pairs={{0,3},{1,2},{2,1},{3,0},{4,7},{5,6},{6,5},{7,4},{8,11},{9,10},{10,... | collective-permute-start | bytes 294920 | tf_op jit(solution)/shard_map/ppermute | solution.py:331
  68.2 3.6 %collective-permute-start.13 = (bf16[8,16,256]{2,1,0:T(8,128)(2,1)S(1)}, bf16[8,16,256]{2,1,0:T(8,128)(2,1)S(1)}, u32[]{:S(2)}, u32[]{:S(2)}) collective-permute-start(bf16[8,16,256]{2,1,0:T(8,128)(2,1)S(1)} %get-tuple-element.86), channel_id=1, source_target_pairs={{0,1},{1,0},{2,3},{3,2},{4,5},{5,4},{6,7},{7,6},{8,9},{9,8},{10,11... | collective-permute-start | bytes 196616 | tf_op jit(solution)/shard_map/ppermute | solution.py:331
  68.3 5.2 %collective-permute-start.14 = (bf16[8,16,256]{2,1,0:T(8,128)(2,1)S(1)}, bf16[8,16,256]{2,1,0:T(8,128)(2,1)S(1)}, u32[]{:S(2)}, u32[]{:S(2)}) collective-permute-start(bf16[8,16,256]{2,1,0:T(8,128)(2,1)S(1)} %get-tuple-element.87), channel_id=1, source_target_pairs={{0,2},{1,3},{2,0},{3,1},{4,6},{5,7},{6,4},{7,5},{8,10},{9,11},{10,... | collective-permute-start | bytes 196616 | tf_op jit(solution)/shard_map/ppermute | solution.py:331
  69.9 4.4 %collective-permute-start.15 = (bf16[8,16,256]{2,1,0:T(8,128)(2,1)S(1)}, bf16[8,16,256]{2,1,0:T(8,128)(2,1)S(1)}, u32[]{:S(2)}, u32[]{:S(2)}) collective-permute-start(bf16[8,16,256]{2,1,0:T(8,128)(2,1)S(1)} %get-tuple-element.88), channel_id=1, source_target_pairs={{0,3},{1,2},{2,1},{3,0},{4,7},{5,6},{6,5},{7,4},{8,11},{9,10},{10,... | collective-permute-start | bytes 196616 | tf_op jit(solution)/shard_map/ppermute | solution.py:331
  75.4 14.1 %all-to-all-start = ((f32[8,64,128]{2,1,0:T(8,128)}), f32[8,64,128]{2,1,0:T(8,128)S(1)}, u32[]{:S(2)}, u32[]{:S(2)}) async-start(f32[8,64,128]{2,1,0:T(8,128)} %get-tuple-element.91), calls=%async_computation | async-start | bytes 524288 | tf_op jit(solution)/shard_map/all_to_all | solution.py:382
